TPU v7x, 128 devices: a whole 4x4x4 slice. The times are simulated.
128 devices in a mesh: tile: 8 (over x, y_lo), chan: 16 (over y_hi, z, core).
Axes of the slice: x: 4, y: 4 (y_hi: 2, y_lo: 2; y = y_hi * 2 + y_lo), z: 4, core: 2. Of those that a mesh axis runs over, the one named last changes fastest.
Arguments:
- visibilities: float32 [8, 16, 2, 2048], P('tile', 'chan'), may hold values from -6 to 6
- cell_offsets: int32 [8, 16, 2, 2048], P('tile', 'chan'), may hold values from 0 to 1023
- support_index: int32 [8, 16, 2048], P('tile', 'chan'), may hold values from 0 to 3
- w_plane: int32 [8, 16, 2048], P('tile', 'chan'), may hold values from 0 to 15
- live_counts: int32 [8, 16], P('tile', 'chan'), may hold values from 256 to 2048, as said below
Outputs:
- grid: float32 [8192, 2, 1024], P(('tile', 'chan'))
Inputs may be any that keep to these rules, and one draw needn't show every extreme that they name: Slots 0 to live_counts - 1 of a tile and group hold visibilities, the others are empty; some tile and group is full.
All inputs are finite; a program needn't handle non-finite values.
Results may differ from a plain program's by a relative error of at most 0.0037.
Values sent between devices are 32-bit elements; how exact they have to be, the bound alone decides.
A program may use at most 64 MiB of HBM per device.

v0:
```python
import math

import jax
import jax.numpy as jnp
from jax import lax
from jax.sharding import PartitionSpec as P

G = 1024
M = 32
PLANES = 16


BETA = 7.0


def from_behind(x, axis, by):
    count = lax.axis_size(axis)
    pairs = [(i, i + by) for i in range(count) if 0 <= i + by < count]
    return lax.ppermute(x, axis, pairs)


def bessel_zero(value):
    quarter = value * value * 0.25
    term = jnp.ones_like(value)
    total = jnp.ones_like(value)
    for index in range(1, 30):
        term = term * quarter / float(index * index)
        total = total + term
    return total


def kernel_values(distance, half_width, w_coef):
    ratio = distance / half_width
    inside = jnp.abs(ratio) < 1.0
    radius = jnp.sqrt(jnp.maximum(1.0 - ratio * ratio, 0.0))
    bessel = bessel_zero(BETA * radius) / bessel_zero(jnp.float32(BETA))
    taper = jnp.cos(jnp.pi * w_coef * ratio * ratio)
    return jnp.where(inside, bessel * taper, jnp.float32(0.0))


def flatten_groups(vis_block, offset_block, support_block, plane_block, count_block):
    slot_total = vis_block.shape[-1]
    slot_ids = jnp.arange(slot_total, dtype=jnp.int32)
    live = (slot_ids[None, :] < count_block[:, None]).astype(jnp.float32).reshape(-1)
    real_part = vis_block[:, 0].reshape(-1) * live
    imag_part = vis_block[:, 1].reshape(-1) * live
    row_cell = offset_block[:, 0].reshape(-1).astype(jnp.float32)
    col_cell = offset_block[:, 1].reshape(-1).astype(jnp.float32)
    half_width = 8.0 * (support_block.reshape(-1) + 1).astype(jnp.float32)
    w_coef = 0.5 * (plane_block.reshape(-1) + 1).astype(jnp.float32) / PLANES
    return (real_part, imag_part, row_cell, col_cell, half_width, w_coef)


def grid_part(flat, row_start, row_count, width):
    total_vis = flat[0].shape[0]
    block_len = math.gcd(total_vis, 512)
    stacked = tuple((item.reshape(total_vis // block_len, block_len) for item in flat))
    row_pos = (row_start + jnp.arange(row_count, dtype=jnp.int32)).astype(jnp.float32)
    col_pos = jnp.arange(width, dtype=jnp.int32).astype(jnp.float32)

    def step_block(total, values):
        real_part, imag_part, row_cell, col_cell, half_width, w_coef = values
        row_weights = kernel_values(
            row_pos[None, :] - row_cell[:, None], half_width[:, None], w_coef[:, None]
        ).astype(jnp.bfloat16)
        col_kern = kernel_values(
            col_pos[None, :] - col_cell[:, None], half_width[:, None], w_coef[:, None]
        )
        col_weights = jnp.concatenate(
            [real_part[:, None] * col_kern, imag_part[:, None] * col_kern], axis=1
        ).astype(jnp.bfloat16)
        product = lax.dot_general(
            row_weights, col_weights, (((0,), (0,)), ((), ())), preferred_element_type=jnp.float32
        )
        return (total + product, None)

    start_total = jnp.zeros((row_count, 2 * width), jnp.float32)
    total, _ = lax.scan(step_block, start_total, stacked)
    return total.reshape(row_count, 2, width)


def move_edges(high_edge, low_edge):
    left_in = from_behind(high_edge, "tile", 1)
    right_in = from_behind(low_edge, "tile", -1)
    return (left_in, right_in)


def sum_edges(first_edge, second_edge):
    return lax.psum((first_edge, second_edge), "chan")


def per_device(visibilities, cell_offsets, support_index, w_plane, live_counts):
    own_flat = flatten_groups(
        visibilities[0], cell_offsets[0], support_index[0], w_plane[0], live_counts[0]
    )
    share = G // lax.axis_size("chan")
    first_row = lax.axis_index("chan") * share
    owned = lax.psum_scatter(
        grid_part(own_flat, jnp.int32(0), share * lax.axis_size("chan"), G),
        "chan",
        scatter_dimension=0,
        tiled=True,
    )
    low_edge = grid_part(own_flat, -M, M, G)
    high_edge = grid_part(own_flat, G, M, G)
    high_sum, low_sum = sum_edges(high_edge, low_edge)
    left_in, right_in = move_edges(high_sum, low_sum)
    zero_rows = jnp.zeros((share, 2, G), jnp.float32)
    upper = jnp.concatenate([left_in, zero_rows], axis=0)
    upper_part = lax.dynamic_slice_in_dim(upper, jnp.minimum(first_row, M), share, 0)
    lower = jnp.concatenate([zero_rows, right_in], axis=0)
    lower_start = jnp.clip(first_row - (G - M - share), 0, M)
    lower_part = lax.dynamic_slice_in_dim(lower, lower_start, share, 0)
    return owned + upper_part + lower_part


def solution(mesh):
    in_specs = (
        P("tile", "chan", None, None),
        P("tile", "chan", None, None),
        P("tile", "chan", None),
        P("tile", "chan", None),
        P("tile", "chan"),
    )
    out_specs = P(("tile", "chan"), None, None)
    return jax.shard_map(
        per_device, mesh=mesh, in_specs=in_specs, out_specs=out_specs, check_vma=False
    )
```

profile of v0, /device:TPU:8, one launch (start us, length us, event | category | flops | bytes accessed | tf_op | source)
XLA Modules:
  0.0 521.2 jit_solution(4775475425677353248)
XLA Ops:
  9.0 158.7 %while.37 = (s32[]{:T(128)}, f32[1024,2048]{1,0:T(8,128)}, f32[4,512]{1,0:T(4,128)S(1)}, f32[4,512]{1,0:T(4,128)S(1)}, f32[4,512]{1,0:T(4,128)S(1)}, /*index=5*/...) while((s32[]{:T(128)}, f32[1024,2048]{1,0:T(8,128)}, ...), condition=%wide.region_1.2_spmd.clone.clone, body=%wide.region_0.1_spmd.clone.clone.sunk | while | flops 2263352832 | bytes 21024888 | solution.py:78
  9.0 17.4 %multiply_convert_fusion.11 = (bf16[512,1024]{1,0:T(8,128)(2,1)S(1)}, bf16[512,1024]{1,0:T(8,128)(2,1)S(1)}) fusion(f32[512]{0:T(512)S(1)} %bitcast.76, f32[512]{0:T(512)S(1)} %bitcast.68, f32[512]{0:T(512)S(1)} %bitcast.70, f32[512]{0:T(512)S(1)} %bitcast.75, f32[1024]{0:T(1024)S(1)} %iota_convert_fusion.8, f32[512]{0:T(512)S(1)} %bitcast.72), kind=kLoop, calls=%fused_computation.207.clone.1 | loop fusion | flops 54525952 | bytes 2111488 | tf_op jit(solution)/shard_map/convert.4
  26.5 20.6 %select_add_fusion.2 = f32[1024,2048]{1,0:T(8,128)} fusion(f32[1024,2048]{1,0:T(8,128)} %get-tuple-element.648, pred[]{:T(512)S(6)} %compare.13, bf16[512,1024]{1,0:T(8,128)(2,1)S(1)} %get-tuple-element.574, bf16[512,1024]{1,0:T(8,128)(2,1)S(1)} %get-tuple-element.575, f32[512]{0:T(512)S(1)} %bitcast.69, f32[512]{0:T(512)S(1)} %bitcast.71, ...), kind=kOutput, calls=%fused_computation.193.clone.1 | convolution fusion | flops 2208825344 | bytes 18884608 | tf_op jit(solution)/shard_map/while/body/eval_jaxpr/dot_general | solution.py:72
  47.1 17.4 %multiply_convert_fusion.11 = (bf16[512,1024]{1,0:T(8,128)(2,1)S(1)}, bf16[512,1024]{1,0:T(8,128)(2,1)S(1)}) fusion(f32[512]{0:T(512)S(1)} %bitcast.76, f32[512]{0:T(512)S(1)} %bitcast.68, f32[512]{0:T(512)S(1)} %bitcast.70, f32[512]{0:T(512)S(1)} %bitcast.75, f32[1024]{0:T(1024)S(1)} %iota_convert_fusion.8, f32[512]{0:T(512)S(1)} %bitcast.72), kind=kLoop, calls=%fused_computation.207.clone.1 | loop fusion | flops 54525952 | bytes 2111488 | tf_op jit(solution)/shard_map/convert.4
  64.5 22.7 %select_add_fusion.2 = f32[1024,2048]{1,0:T(8,128)} fusion(f32[1024,2048]{1,0:T(8,128)} %get-tuple-element.648, pred[]{:T(512)S(6)} %compare.13, bf16[512,1024]{1,0:T(8,128)(2,1)S(1)} %get-tuple-element.574, bf16[512,1024]{1,0:T(8,128)(2,1)S(1)} %get-tuple-element.575, f32[512]{0:T(512)S(1)} %bitcast.69, f32[512]{0:T(512)S(1)} %bitcast.71, ...), kind=kOutput, calls=%fused_computation.193.clone.1 | convolution fusion | flops 2208825344 | bytes 18884608 | tf_op jit(solution)/shard_map/while/body/eval_jaxpr/dot_general | solution.py:72
  87.3 17.4 %multiply_convert_fusion.11 = (bf16[512,1024]{1,0:T(8,128)(2,1)S(1)}, bf16[512,1024]{1,0:T(8,128)(2,1)S(1)}) fusion(f32[512]{0:T(512)S(1)} %bitcast.76, f32[512]{0:T(512)S(1)} %bitcast.68, f32[512]{0:T(512)S(1)} %bitcast.70, f32[512]{0:T(512)S(1)} %bitcast.75, f32[1024]{0:T(1024)S(1)} %iota_convert_fusion.8, f32[512]{0:T(512)S(1)} %bitcast.72), kind=kLoop, calls=%fused_computation.207.clone.1 | loop fusion | flops 54525952 | bytes 2111488 | tf_op jit(solution)/shard_map/convert.4
  104.7 22.7 %select_add_fusion.2 = f32[1024,2048]{1,0:T(8,128)} fusion(f32[1024,2048]{1,0:T(8,128)} %get-tuple-element.648, pred[]{:T(512)S(6)} %compare.13, bf16[512,1024]{1,0:T(8,128)(2,1)S(1)} %get-tuple-element.574, bf16[512,1024]{1,0:T(8,128)(2,1)S(1)} %get-tuple-element.575, f32[512]{0:T(512)S(1)} %bitcast.69, f32[512]{0:T(512)S(1)} %bitcast.71, ...), kind=kOutput, calls=%fused_computation.193.clone.1 | convolution fusion | flops 2208825344 | bytes 18884608 | tf_op jit(solution)/shard_map/while/body/eval_jaxpr/dot_general | solution.py:72
  127.5 17.4 %multiply_convert_fusion.11 = (bf16[512,1024]{1,0:T(8,128)(2,1)S(1)}, bf16[512,1024]{1,0:T(8,128)(2,1)S(1)}) fusion(f32[512]{0:T(512)S(1)} %bitcast.76, f32[512]{0:T(512)S(1)} %bitcast.68, f32[512]{0:T(512)S(1)} %bitcast.70, f32[512]{0:T(512)S(1)} %bitcast.75, f32[1024]{0:T(1024)S(1)} %iota_convert_fusion.8, f32[512]{0:T(512)S(1)} %bitcast.72), kind=kLoop, calls=%fused_computation.207.clone.1 | loop fusion | flops 54525952 | bytes 2111488 | tf_op jit(solution)/shard_map/convert.4
  144.9 22.7 %select_add_fusion.2 = f32[1024,2048]{1,0:T(8,128)} fusion(f32[1024,2048]{1,0:T(8,128)} %get-tuple-element.648, pred[]{:T(512)S(6)} %compare.13, bf16[512,1024]{1,0:T(8,128)(2,1)S(1)} %get-tuple-element.574, bf16[512,1024]{1,0:T(8,128)(2,1)S(1)} %get-tuple-element.575, f32[512]{0:T(512)S(1)} %bitcast.69, f32[512]{0:T(512)S(1)} %bitcast.71, ...), kind=kOutput, calls=%fused_computation.193.clone.1 | convolution fusion | flops 2208825344 | bytes 18884608 | tf_op jit(solution)/shard_map/while/body/eval_jaxpr/dot_general | solution.py:72
  167.6 11.7 %reshape.119 = f32[1024,2,1024]{2,1,0:T(2,128)} reshape(f32[1024,2048]{1,0:T(8,128)} %get-tuple-element.183) | data formatting | bytes 16777216 | tf_op jit(solution)/shard_map/reshape | solution.py:79
  179.4 74.5 %while.36 = (s32[]{:T(128)}, f32[32,2048]{1,0:T(8,128)S(1)}, f32[4,512]{1,0:T(4,128)S(1)}, f32[4,512]{1,0:T(4,128)S(1)}, f32[4,512]{1,0:T(4,128)S(1)}, /*index=5...) while((s32[]{:T(128)}, f32[32,2048]{1,0:T(8,128)S(1)}, ...), condition=%wide.region_7.8_spmd.clone, body=%wide.region_6.7_spmd.clone.sunk | while | flops 127616576 | bytes 4768123 | solution.py:78
  179.4 17.4 %multiply_convert_fusion.10 = (bf16[512,1024]{1,0:T(8,128)(2,1)S(1)}, bf16[512,1024]{1,0:T(8,128)(2,1)S(1)}) fusion(f32[512]{0:T(512)S(1)} %bitcast.60, f32[512]{0:T(512)S(1)} %bitcast.64, f32[512]{0:T(512)S(1)} %bitcast.77, f32[1024]{0:T(1024)S(1)} %iota_convert_fusion.7, f32[512]{0:T(512)S(1)} %bitcast.78, f32[512]{0:T(512)S(1)} %bitcast.73), kind=kLoop, calls=%fused_computation.108.clone.1 | loop fusion | flops 54525952 | bytes 2111488 | tf_op jit(solution)/shard_map/convert
  198.1 17.4 %multiply_convert_fusion.10 = (bf16[512,1024]{1,0:T(8,128)(2,1)S(1)}, bf16[512,1024]{1,0:T(8,128)(2,1)S(1)}) fusion(f32[512]{0:T(512)S(1)} %bitcast.60, f32[512]{0:T(512)S(1)} %bitcast.64, f32[512]{0:T(512)S(1)} %bitcast.77, f32[1024]{0:T(1024)S(1)} %iota_convert_fusion.7, f32[512]{0:T(512)S(1)} %bitcast.78, f32[512]{0:T(512)S(1)} %bitcast.73), kind=kLoop, calls=%fused_computation.108.clone.1 | loop fusion | flops 54525952 | bytes 2111488 | tf_op jit(solution)/shard_map/convert
  216.7 17.4 %multiply_convert_fusion.10 = (bf16[512,1024]{1,0:T(8,128)(2,1)S(1)}, bf16[512,1024]{1,0:T(8,128)(2,1)S(1)}) fusion(f32[512]{0:T(512)S(1)} %bitcast.60, f32[512]{0:T(512)S(1)} %bitcast.64, f32[512]{0:T(512)S(1)} %bitcast.77, f32[1024]{0:T(1024)S(1)} %iota_convert_fusion.7, f32[512]{0:T(512)S(1)} %bitcast.78, f32[512]{0:T(512)S(1)} %bitcast.73), kind=kLoop, calls=%fused_computation.108.clone.1 | loop fusion | flops 54525952 | bytes 2111488 | tf_op jit(solution)/shard_map/convert
  235.3 17.4 %multiply_convert_fusion.10 = (bf16[512,1024]{1,0:T(8,128)(2,1)S(1)}, bf16[512,1024]{1,0:T(8,128)(2,1)S(1)}) fusion(f32[512]{0:T(512)S(1)} %bitcast.60, f32[512]{0:T(512)S(1)} %bitcast.64, f32[512]{0:T(512)S(1)} %bitcast.77, f32[1024]{0:T(1024)S(1)} %iota_convert_fusion.7, f32[512]{0:T(512)S(1)} %bitcast.78, f32[512]{0:T(512)S(1)} %bitcast.73), kind=kLoop, calls=%fused_computation.108.clone.1 | loop fusion | flops 54525952 | bytes 2111488 | tf_op jit(solution)/shard_map/convert
  254.8 74.4 %while.35 = (s32[]{:T(128)}, f32[32,2048]{1,0:T(8,128)S(1)}, f32[4,512]{1,0:T(4,128)S(1)}, f32[4,512]{1,0:T(4,128)S(1)}, f32[4,512]{1,0:T(4,128)S(1)}, /*index=5...) while((s32[]{:T(128)}, f32[32,2048]{1,0:T(8,128)S(1)}, ...), condition=%wide.region_4.5_spmd.clone, body=%wide.region_3.4_spmd.clone.sunk | while | flops 127616576 | bytes 4768123 | solution.py:78
  254.8 17.4 %multiply_convert_fusion.9 = (bf16[512,1024]{1,0:T(8,128)(2,1)S(1)}, bf16[512,1024]{1,0:T(8,128)(2,1)S(1)}) fusion(f32[512]{0:T(512)S(1)} %bitcast.62, f32[512]{0:T(512)S(1)} %bitcast.66, f32[512]{0:T(512)S(1)} %bitcast.79, f32[1024]{0:T(1024)S(1)} %iota_convert_fusion.6, f32[512]{0:T(512)S(1)} %bitcast.80, f32[512]{0:T(512)S(1)} %bitcast.74), kind=kLoop, calls=%fused_computation.14.clone.1 | loop fusion | flops 54525952 | bytes 2111488 | tf_op jit(solution)/shard_map/convert.2
  273.4 17.4 %multiply_convert_fusion.9 = (bf16[512,1024]{1,0:T(8,128)(2,1)S(1)}, bf16[512,1024]{1,0:T(8,128)(2,1)S(1)}) fusion(f32[512]{0:T(512)S(1)} %bitcast.62, f32[512]{0:T(512)S(1)} %bitcast.66, f32[512]{0:T(512)S(1)} %bitcast.79, f32[1024]{0:T(1024)S(1)} %iota_convert_fusion.6, f32[512]{0:T(512)S(1)} %bitcast.80, f32[512]{0:T(512)S(1)} %bitcast.74), kind=kLoop, calls=%fused_computation.14.clone.1 | loop fusion | flops 54525952 | bytes 2111488 | tf_op jit(solution)/shard_map/convert.2
  292.0 17.4 %multiply_convert_fusion.9 = (bf16[512,1024]{1,0:T(8,128)(2,1)S(1)}, bf16[512,1024]{1,0:T(8,128)(2,1)S(1)}) fusion(f32[512]{0:T(512)S(1)} %bitcast.62, f32[512]{0:T(512)S(1)} %bitcast.66, f32[512]{0:T(512)S(1)} %bitcast.79, f32[1024]{0:T(1024)S(1)} %iota_convert_fusion.6, f32[512]{0:T(512)S(1)} %bitcast.80, f32[512]{0:T(512)S(1)} %bitcast.74), kind=kLoop, calls=%fused_computation.14.clone.1 | loop fusion | flops 54525952 | bytes 2111488 | tf_op jit(solution)/shard_map/convert.2
  310.6 17.4 %multiply_convert_fusion.9 = (bf16[512,1024]{1,0:T(8,128)(2,1)S(1)}, bf16[512,1024]{1,0:T(8,128)(2,1)S(1)}) fusion(f32[512]{0:T(512)S(1)} %bitcast.62, f32[512]{0:T(512)S(1)} %bitcast.66, f32[512]{0:T(512)S(1)} %bitcast.79, f32[1024]{0:T(1024)S(1)} %iota_convert_fusion.6, f32[512]{0:T(512)S(1)} %bitcast.80, f32[512]{0:T(512)S(1)} %bitcast.74), kind=kLoop, calls=%fused_computation.14.clone.1 | loop fusion | flops 54525952 | bytes 2111488 | tf_op jit(solution)/shard_map/convert.2
  330.1 167.5 %all-reduce.6.cloned.1.call-done = (f32[32,2,1024]{2,1,0:T(2,128)}, f32[32,2,1024]{2,1,0:T(2,128)}, f32[1024,2,1024]{2,1,0:T(2,128)}) async-done(((f32[32,2,1024]{2,1,0:T(2,128)}, f32[32,2,1024]{2,1,0:T(2,128)}, f32[1024,2,1024]{2,1,0:T(2,128)}), (f32[32,2,1024]{2,1,0:T(2,128)}, f32[32,2,1024]{2,1,0:T(2,128)}, f32[1024,2,1024]{2,1,0:T(2,128)})) %all-reduce.6.cloned.1.call-update) | async-done | bytes 8912912 | tf_op jit(solution)/shard_map/psum | solution.py:89
  497.6 4.2 collective-permute-start
  505.0 6.7 %collective-permute-done = f32[32,2,1024]{2,1,0:T(2,128)S(1)} collective-permute-done((f32[32,2,1024]{2,1,0:T(2,128)}, f32[32,2,1024]{2,1,0:T(2,128)S(1)}, u32[]{:S(2)}, u32[]{:S(2)}) %collective-permute-start) | collective-permute-done | bytes 262176 | tf_op jit(solution)/shard_map/ppermute | solution.py:19
  511.7 2.6 fusion.251
  (86 shorter events, 15.3 us)
Async XLA Ops:
  6.5 491.1 %all-reduce.6.cloned.1.call-start = ((), (), s32[]{:S(2)}) async-start(), calls=%async_computation | async-start | bytes 17825792 | tf_op jit(solution)/shard_map/psum | solution.py:89
  330.1 173.7 %copy-start = (u32[128]{0:T(128)S(1)}, u32[128]{0:T(128)}, u32[]{:S(2)}) copy-start(u32[128]{0:T(128)} %constant.564) | copy-start | bytes 1540
  497.6 14.1 %collective-permute-start = (f32[32,2,1024]{2,1,0:T(2,128)}, f32[32,2,1024]{2,1,0:T(2,128)S(1)}, u32[]{:S(2)}, u32[]{:S(2)}) collective-permute-start(f32[32,2,1024]{2,1,0:T(2,128)} %get-tuple-element.351), channel_id=1, source_target_pairs={{0,16},{16,32},{32,48},{48,64},{64,80},{80,96},{96,112},{1,17},{17... | collective-permute-start | bytes 786440 | tf_op jit(solution)/shard_map/ppermute | solution.py:19
  501.8 9.9 %collective-permute-start.1 = (f32[32,2,1024]{2,1,0:T(2,128)}, f32[32,2,1024]{2,1,0:T(2,128)S(1)}, u32[]{:S(2)}, u32[]{:S(2)}) collective-permute-start(f32[32,2,1024]{2,1,0:T(2,128)} %get-tuple-element.352), channel_id=1, source_target_pairs={{16,0},{32,16},{48,32},{64,48},{80,64},{96,80},{112,96},{17,1},{33... | collective-permute-start | bytes 786440 | tf_op jit(solution)/shard_map/ppermute | solution.py:19
Sparse Core Ops, SparseCore 0:
  330.2 167.2 all-reduce.5
where the time goes:
time: 524 us; the launch traced here: 521 us
  other arithmetic  213 us (41%)
  waiting for transfers between devices  174 us (33%)
  matrix products  97.4 us (19%)
  between operations  14.8 us (3%)
  local copies, waits for them, and re-layouts  14.5 us (3%)
  starting transfers between devices  6.16 us (1%)
    another operation x12, other arithmetic  209 us
    psum x1, waiting for transfers between devices, sum_edges(): return lax.psum((first_edge, second_edge), 'chan')  167 us
    dot_general x12, matrix products, step_block(): lax.dot_general(row_weights, col_weights, (((0,), (0,)), ((), ())), prefe...  97.4 us
    reshape x3, local copies, waits for them, and re-layouts, grid_part(): return total.reshape(row_count, 2, width)  13.6 us
  transfers between devices with their start and end apart: 3, of which 2 were waited for; matrix products, arithmetic and copies ran while one was open for 0% of the time, Pallas kernels for 0%

commit v1 on v0

--- a/solution.py
+++ b/solution.py
@@ -1,16 +1,26 @@
+import functools
 import math
 
 import jax
 import jax.numpy as jnp
 from jax import lax
+from jax.experimental import pallas as pl
+from jax.experimental.pallas import tpu as pltpu
 from jax.sharding import PartitionSpec as P
 
 G = 1024
 M = 32
 PLANES = 16
-
-
 BETA = 7.0
+
+BUCKET = 32
+CAP = 128
+LOW = 32
+GROUPS_IN = CAP // LOW
+FIELDS = 8
+MESH = pl.DeviceIdType.MESH
+F32 = jnp.float32
+BF16 = jnp.bfloat16
 
 
 def from_behind(x, axis, by):
@@ -24,7 +34,7 @@
     term = jnp.ones_like(value)
     total = jnp.ones_like(value)
     for index in range(1, 30):
-        term = term * quarter / float(index * index)
+        term = term * quarter * (1.0 / float(index * index))
         total = total + term
     return total
 
@@ -79,17 +89,7 @@
     return total.reshape(row_count, 2, width)
 
 
-def move_edges(high_edge, low_edge):
-    left_in = from_behind(high_edge, "tile", 1)
-    right_in = from_behind(low_edge, "tile", -1)
-    return (left_in, right_in)
-
-
-def sum_edges(first_edge, second_edge):
-    return lax.psum((first_edge, second_edge), "chan")
-
-
-def per_device(visibilities, cell_offsets, support_index, w_plane, live_counts):
+def any_cells(visibilities, cell_offsets, support_index, w_plane, live_counts):
     own_flat = flatten_groups(
         visibilities[0], cell_offsets[0], support_index[0], w_plane[0], live_counts[0]
     )
@@ -103,8 +103,9 @@
     )
     low_edge = grid_part(own_flat, -M, M, G)
     high_edge = grid_part(own_flat, G, M, G)
-    high_sum, low_sum = sum_edges(high_edge, low_edge)
-    left_in, right_in = move_edges(high_sum, low_sum)
+    high_sum, low_sum = lax.psum((high_edge, low_edge), "chan")
+    left_in = from_behind(high_sum, "tile", 1)
+    right_in = from_behind(low_sum, "tile", -1)
     zero_rows = jnp.zeros((share, 2, G), jnp.float32)
     upper = jnp.concatenate([left_in, zero_rows], axis=0)
     upper_part = lax.dynamic_slice_in_dim(upper, jnp.minimum(first_row, M), share, 0)
@@ -112,6 +113,289 @@
     lower_start = jnp.clip(first_row - (G - M - share), 0, M)
     lower_part = lax.dynamic_slice_in_dim(lower, lower_start, share, 0)
     return owned + upper_part + lower_part
+
+
+def class_table():
+    klass = lax.broadcasted_iota(jnp.int32, (128, 128), 0)
+    distance = lax.broadcasted_iota(jnp.int32, (128, 128), 1).astype(F32)
+    half = (8 * (klass // PLANES + 1)).astype(F32)
+    w_coef = 0.5 * (klass % PLANES + 1).astype(F32) / PLANES
+    ratio = distance / half
+    inside = (ratio < 1.0) & (klass < 4 * PLANES)
+    bound = jnp.minimum(ratio, 1.0)
+    square = bound * bound
+    radius = jnp.sqrt(jnp.maximum(1.0 - square, 0.0))
+    bessel = bessel_zero(BETA * radius) / bessel_zero(jnp.full((128, 128), BETA, F32))
+    taper = jnp.cos(jnp.pi * w_coef * square)
+    return jnp.where(inside, bessel * taper, 0.0)
+
+
+def exchange(vis, cell, sup, wpl, cnt, got, edge, table, flag, vis_v, cell_v, sup_v, wpl_v, packed, tile_flags, chan_flags,
+             load_sem, send_sem, recv_sem, edge_send, edge_recv, tf_send, tf_recv, cf_send, cf_recv):
+    t, c = lax.axis_index("tile"), lax.axis_index("chan")
+    nt, nc = lax.axis_size("tile"), lax.axis_size("chan")
+    slots = vis_v.shape[-1]
+    loads = [
+        pltpu.make_async_copy(vis.at[0, 0], vis_v, load_sem.at[0]),
+        pltpu.make_async_copy(cell.at[0, 0], cell_v, load_sem.at[1]),
+        pltpu.make_async_copy(sup.at[0], sup_v, load_sem.at[2]),
+        pltpu.make_async_copy(wpl.at[0], wpl_v, load_sem.at[3]),
+    ]
+    for load in loads:
+        load.start()
+    edge[...] = jnp.zeros_like(edge)
+
+    bar = pltpu.get_barrier_semaphore()
+    for i in range(1, nc):
+        pl.semaphore_signal(bar, inc=1, device_id=(t, lax.rem(c + i, nc)), device_id_type=MESH)
+    for i in range(1, nt):
+        pl.semaphore_signal(bar, inc=1, device_id=(lax.rem(t + i, nt), c), device_id_type=MESH)
+    from_low = (c == 0) & (t > 0)
+    from_high = (c == nc - 1) & (t < nt - 1)
+
+    @pl.when(from_low)
+    def _():
+        for g in range(nc):
+            pl.semaphore_signal(bar, inc=1, device_id=(t - 1, g), device_id_type=MESH)
+
+    @pl.when(from_high)
+    def _():
+        for g in range(nc):
+            pl.semaphore_signal(bar, inc=1, device_id=(t + 1, g), device_id_type=MESH)
+
+    for load in loads:
+        load.wait()
+
+    live = lax.broadcasted_iota(jnp.int32, (1, slots), 1) < cnt[0, 0]
+    row = cell_v[0:1]
+    bucket = jnp.where(live, row // BUCKET, -1)
+    buckets = G // BUCKET
+    hot = (lax.broadcasted_iota(jnp.int32, (buckets, slots), 0) == bucket).astype(F32)
+    step = 256
+    before = (
+        lax.broadcasted_iota(jnp.int32, (step, step), 0) < lax.broadcasted_iota(jnp.int32, (step, step), 1)
+    ).astype(F32).astype(BF16)
+    parts = []
+    carry = jnp.zeros((buckets, 1), F32)
+    for s in range(0, slots, step):
+        piece = hot[:, s : s + step]
+        ahead = jnp.dot(piece.astype(BF16), before, preferred_element_type=F32) + carry
+        parts.append(jnp.sum(piece * ahead, axis=0, keepdims=True))
+        carry = carry + jnp.sum(piece, axis=1, keepdims=True)
+    rank = jnp.concatenate(parts, axis=1).astype(jnp.int32)
+    over = (jnp.max(carry, axis=0, keepdims=True) > CAP).astype(F32)
+    tile_flags[t] = jnp.broadcast_to(over, (8, 128))
+
+    group = jnp.where(live, (bucket + 1) * GROUPS_IN + rank // LOW, -1)
+    place = rank % LOW
+    groups = packed.shape[0]
+    to_group = (lax.broadcasted_iota(jnp.int32, (groups, slots), 0) == group).astype(F32).astype(BF16)
+    at_place = lax.broadcasted_iota(jnp.int32, (LOW, slots), 0) == place
+
+    def halves(x):
+        high = x.astype(BF16).astype(F32)
+        return high, x - high
+
+    re_hi, re_lo = halves(vis_v[0:1])
+    im_hi, im_lo = halves(vis_v[1:2])
+    col_hi, col_lo = halves(cell_v[1:2].astype(F32))
+    pieces = [re_hi, im_hi, col_hi, (row % BUCKET).astype(F32), sup_v[...].astype(F32), wpl_v[...].astype(F32),
+              jnp.ones((1, slots), F32), jnp.zeros((1, slots), F32), re_lo, im_lo, col_lo, jnp.zeros((1, slots), F32)]
+    spread = jnp.concatenate([jnp.where(at_place, x, 0.0).astype(BF16) for x in pieces], axis=0)
+    moved = lax.dot_general(to_group, spread, (((1,), (1,)), ((), ())), preferred_element_type=F32)
+    packed[:, 0:128] = moved[:, 0:128] + moved[:, 256:384]
+    packed[:, 128:256] = moved[:, 128:256]
+
+    below, above = (t > 0).astype(jnp.int32), (t < nt - 1).astype(jnp.int32)
+    pl.semaphore_wait(bar, nc - 1 + nt - 1 + below + above)
+
+    def tile_flag(i, slot):
+        return pltpu.make_async_remote_copy(
+            src_ref=tile_flags.at[t], dst_ref=tile_flags.at[slot], send_sem=tf_send.at[i], recv_sem=tf_recv.at[slot],
+            device_id=(lax.rem(t + i, nt), c), device_id_type=MESH)
+
+    for i in range(1, nt):
+        tile_flag(i, t).start()
+
+    width = 4 * GROUPS_IN
+
+    def payload(i, slot):
+        peer = lax.rem(c + i, nc)
+        return pltpu.make_async_remote_copy(
+            src_ref=packed.at[pl.ds(pl.multiple_of(8 * peer, 8), width)], dst_ref=got.at[slot], send_sem=send_sem.at[i],
+            recv_sem=recv_sem.at[slot], device_id=(t, peer), device_id_type=MESH)
+
+    order = [8, 7, 9, 6, 10, 5, 11, 4, 12, 3, 13, 2, 14, 1, 15]
+    for i in order:
+        payload(i, c).start()
+
+    def edge_up():
+        return pltpu.make_async_remote_copy(
+            src_ref=packed.at[pl.ds(buckets * GROUPS_IN, GROUPS_IN)], dst_ref=edge.at[c, 0:GROUPS_IN], send_sem=edge_send.at[0],
+            recv_sem=edge_recv.at[c], device_id=(t + 1, 0), device_id_type=MESH)
+
+    def edge_down():
+        return pltpu.make_async_remote_copy(
+            src_ref=packed.at[pl.ds(GROUPS_IN, GROUPS_IN)], dst_ref=edge.at[c, 0:GROUPS_IN], send_sem=edge_send.at[1],
+            recv_sem=edge_recv.at[c], device_id=(t - 1, nc - 1), device_id_type=MESH)
+
+    @pl.when(t < nt - 1)
+    def _():
+        edge_up().start()
+
+    @pl.when(t > 0)
+    def _():
+        edge_down().start()
+
+    got[c] = packed[pl.ds(pl.multiple_of(8 * c, 8), width), :]
+
+    for i in range(1, nt):
+        tile_flag(i, lax.rem(t + i, nt)).wait_recv()
+    chan_flags[c] = jnp.max(tile_flags[...], axis=0)
+
+    def chan_flag(i, slot):
+        return pltpu.make_async_remote_copy(
+            src_ref=chan_flags.at[c], dst_ref=chan_flags.at[slot], send_sem=cf_send.at[i], recv_sem=cf_recv.at[slot],
+            device_id=(t, lax.rem(c + i, nc)), device_id_type=MESH)
+
+    for i in range(1, nc):
+        chan_flag(i, c).start()
+
+    table[...] = class_table().astype(BF16)
+
+    for i in range(1, nc):
+        payload(i, lax.rem(c + i, nc)).wait_recv()
+
+    @pl.when(from_low | from_high)
+    def _():
+        for g in range(nc):
+            pltpu.make_async_remote_copy(
+                src_ref=packed.at[pl.ds(0, GROUPS_IN)], dst_ref=edge.at[g, 0:GROUPS_IN], send_sem=edge_send.at[0],
+                recv_sem=edge_recv.at[g], device_id=(t, g), device_id_type=MESH).wait_recv()
+
+    for i in range(1, nc):
+        chan_flag(i, lax.rem(c + i, nc)).wait_recv()
+    flag[...] = jnp.max(chan_flags[...], axis=0)
+    for i in range(1, nt):
+        tile_flag(i, t).wait_send()
+    for i in range(1, nc):
+        payload(i, c).wait_send()
+        chan_flag(i, c).wait_send()
+
+    @pl.when(t < nt - 1)
+    def _():
+        edge_up().wait_send()
+
+    @pl.when(t > 0)
+    def _():
+        edge_down().wait_send()
+
+
+def owned_rows(got, edge, table, out, rows, total):
+    c = lax.axis_index("chan")
+    nc = got.shape[0]
+    per = got.shape[1]
+    main = nc * per
+    count = main + nc * 8
+
+    lanes = lax.broadcasted_iota(jnp.int32, (1, 256), 1) // LOW
+    both = jnp.concatenate([got[...].reshape(main, 256), edge[...].reshape(nc * 8, 256)], axis=0)
+    index = lax.broadcasted_iota(jnp.int32, (count, 256), 0)
+    shift = jnp.where(index < main, BUCKET * ((index % per) // GROUPS_IN - 1), jnp.where(c == 0, -BUCKET, 2 * BUCKET))
+    both = both + jnp.where(lanes == 3, shift, 0).astype(F32)
+    used = jnp.where(lax.broadcasted_iota(jnp.int32, (128, count), 0) == 6 * LOW - 128, both[:, 128:256].T, 0.0)
+    used = jnp.sum(used, axis=0, keepdims=True)
+    before = (
+        lax.broadcasted_iota(jnp.int32, (count, count), 0) < lax.broadcasted_iota(jnp.int32, (count, count), 1)
+    ).astype(F32).astype(BF16)
+    rank = jnp.dot(jnp.broadcast_to(used, (8, count)).astype(BF16), before, preferred_element_type=F32)[0:1]
+    pick = jnp.where(
+        (lax.broadcasted_iota(jnp.int32, (count, count), 0).astype(F32) == rank) & (used > 0.5), 1.0, 0.0
+    ).astype(BF16)
+    high = both.astype(BF16)
+    low = (both - high.astype(F32)).astype(BF16)
+    rows[...] = jnp.dot(pick, high, preferred_element_type=F32) + jnp.dot(pick, low, preferred_element_type=F32)
+    trips = (jnp.sum(used).astype(jnp.int32) + 7) // 8
+
+    total[...] = jnp.zeros_like(total)
+    lane = lax.broadcasted_iota(jnp.int32, (256, 128), 1)
+
+    def body(i, carry):
+        block = rows[pl.ds(pl.multiple_of(8 * i, 8), 8), :]
+        klass = block[:, 128 : 128 + LOW] * float(PLANES) + block[:, 128 + LOW : 128 + 2 * LOW]
+        first = block[:, 0:128].T
+        second = jnp.concatenate([klass, block[:, 128 + LOW : 256]], axis=1).T
+
+        def field(x, f):
+            return jnp.concatenate(
+                [jnp.broadcast_to(x[f * LOW : (f + 1) * LOW, r : r + 1], (LOW, 128)) for r in range(8)], axis=0)
+
+        re, im = field(first, 0), field(first, 1)
+        col, row = field(first, 2).astype(jnp.int32), field(first, 3).astype(jnp.int32)
+        hot = (field(second, 0).astype(jnp.int32) == lane).astype(F32).astype(BF16)
+        values = jnp.dot(hot, table[...], preferred_element_type=F32)
+
+        def look_up(distance):
+            return jnp.take_along_axis(values, jnp.minimum(jnp.abs(distance), 127), axis=1, mode="promise_in_bounds")
+
+        weights = (look_up(lane // 2 - row) * jnp.where(lane % 2 == 0, re, im)).astype(BF16)
+        columns = jnp.concatenate([look_up(lane + 128 * b - col).astype(BF16) for b in range(G // 128)], axis=1)
+        total[...] += lax.dot_general(weights, columns, (((0,), (0,)), ((), ())), preferred_element_type=F32)
+        return carry
+
+    lax.fori_loop(0, trips, body, 0)
+    out[...] = total[...].reshape(out.shape)
+
+
+def per_device(visibilities, cell_offsets, support_index, w_plane, live_counts):
+    nt, nc = lax.axis_size("tile"), lax.axis_size("chan")
+    slots = visibilities.shape[-1]
+    groups = (G // BUCKET + 2) * GROUPS_IN
+    vmem = pl.BlockSpec(memory_space=pltpu.VMEM)
+    got, edge, table, flag = pl.pallas_call(
+        exchange,
+        out_shape=(
+            jax.ShapeDtypeStruct((nc, 4 * GROUPS_IN, FIELDS * LOW), F32),
+            jax.ShapeDtypeStruct((nc, 8, FIELDS * LOW), F32),
+            jax.ShapeDtypeStruct((128, 128), BF16),
+            jax.ShapeDtypeStruct((8, 128), F32),
+        ),
+        in_specs=[pl.BlockSpec(memory_space=pl.ANY)] * 4 + [pl.BlockSpec(memory_space=pltpu.SMEM)],
+        out_specs=(vmem,) * 4,
+        scratch_shapes=[
+            pltpu.VMEM((2, slots), F32),
+            pltpu.VMEM((2, slots), jnp.int32),
+            pltpu.VMEM((1, slots), jnp.int32),
+            pltpu.VMEM((1, slots), jnp.int32),
+            pltpu.VMEM((groups, FIELDS * LOW), F32),
+            pltpu.VMEM((nt, 8, 128), F32),
+            pltpu.VMEM((nc, 8, 128), F32),
+            pltpu.SemaphoreType.DMA((4,)),
+            pltpu.SemaphoreType.DMA((nc,)),
+            pltpu.SemaphoreType.DMA((nc,)),
+            pltpu.SemaphoreType.DMA((2,)),
+            pltpu.SemaphoreType.DMA((nc,)),
+            pltpu.SemaphoreType.DMA((nt,)),
+            pltpu.SemaphoreType.DMA((nt,)),
+            pltpu.SemaphoreType.DMA((nc,)),
+            pltpu.SemaphoreType.DMA((nc,)),
+        ],
+        compiler_params=pltpu.CompilerParams(collective_id=0, has_side_effects=True, vmem_limit_bytes=62 << 20),
+    )(visibilities, cell_offsets, support_index, w_plane, live_counts)
+
+    def usual(*_):
+        return pl.pallas_call(
+            owned_rows,
+            out_shape=jax.ShapeDtypeStruct((G // nc, 2, G), F32),
+            in_specs=[vmem] * 3,
+            out_specs=vmem,
+            scratch_shapes=[pltpu.VMEM((nc * (4 * GROUPS_IN + 8), FIELDS * LOW), F32), pltpu.VMEM((2 * G // nc, G), F32)],
+            compiler_params=pltpu.CompilerParams(vmem_limit_bytes=40 << 20),
+        )(got, edge, table)
+
+    return lax.cond(
+        flag[0, 0] > 0.5, any_cells, usual, visibilities, cell_offsets, support_index, w_plane, live_counts
+    )
 
 
 def solution(mesh):

time: 524 us -> 57 us (0.11)
  the two profiles are of different devices: /device:TPU:8 before, /device:TPU:1 now
where the time goes in v1:
time: 57 us; the launch traced here: 56.7 us
  Pallas kernels  39.8 us (70%)
  between operations  14.7 us (26%)
  local copies, waits for them, and re-layouts  1.97 us (3%)
    pallas_call x1, Pallas kernels, usual(): pl.pallas_call(owned_rows, out_shape=jax.ShapeDtypeStruct((G // nc, 2, G)...  21.1 us
    pallas_call x1, Pallas kernels, per_device(): pl.pallas_call(exchange, out_shape=(jax.ShapeDtypeStruct((nc, 4 * GROUPS_...  18.7 us
    slice x1, local copies, waits for them, and re-layouts, per_device(): flag[0, 0] > 0.5  1.18 us

profile of v1, /device:TPU:1, one launch (start us, length us, event | category | flops | bytes accessed | tf_op | source)
XLA Modules:
  0.0 56.7 jit_solution(17999656361025790910)
XLA Ops:
  7.2 18.7 %shard_map.57 = (f32[16,16,256]{2,1,0:T(8,128)S(1)}, f32[16,8,256]{2,1,0:T(8,128)S(1)}, bf16[128,128]{1,0:T(8,128)(2,1)S(1)}, f32[8,128]{1,0:T(8,128)}) custom-call(f32[1,1,2,2048]{3,2,1,0:T(2,128)} %vis.1, s32[1,1,2,2048]{3,2,1,0:T(2,128)} %cell.1, s32[1,1,2048]{2,1,0:T(1,128)} %sup.1, s32[1,1,2048]{2,1,0:T(1,128)} %wpl.1, s32[1,1]{1,0:T(1,128)S(6)} %copy.31.cnt), custom_call_target="tpu_custom_call" | custom-call | tf_op jit(solution)/shard_map/pallas_call | solution.py:355
  25.8 1.2 %slice.15 = f32[1,1]{1,0:T(1,128)} slice(f32[8,128]{1,0:T(8,128)} %get-tuple-element.214), slice={[0:1], [0:1]} | slice | bytes 8 | tf_op jit(solution)/shard_map/slice | solution.py:397
  27.7 21.4 %conditional.1 = (f32[64,2,1024]{2,1,0:T(2,128)S(1)}) conditional(s32[]{:T(128)} %bitcast.3, (f32[16,16,256]{2,1,0:T(8,128)S(1)}, f32[16,8,256]{2,1,0:T(8,128)S(1)}, bf16[128,128]{1,0:T(8,128)(2,1)S(1)}) %tuple.26, (s32[1,1]{1,0:T(1,128)}, f32[1,1,2,2048]{3,2,1,0:T(2,128)}, s32[1,1,2,2048]{3,2,1,0:T(2,128)}, s32[1,1,2048]{2,1,0:T(1,128)}, ...), branch_computations={%region_0.0_spmd, %region_1.11_spmd} | conditional | flops 2521108992 | bytes 105766376 | solution.py:396
  27.7 21.1 %branch_0_fun.1 = f32[64,2,1024]{2,1,0:T(2,128)S(1)} custom-call(f32[16,16,256]{2,1,0:T(8,128)S(1)} %get-tuple-element.166.got, f32[16,8,256]{2,1,0:T(8,128)S(1)} %get-tuple-element.167.edge, bf16[128,128]{1,0:T(8,128)(2,1)S(1)} %get-tuple-element.168.table), custom_call_target="tpu_custom_call" | custom-call | tf_op jit(solution)/shard_map/cond/branch_0_fun/pallas_call | solution.py:387
  49.1 0.0 copy-start
  49.1 0.8 %copy-done = f32[64,2,1024]{2,1,0:T(2,128)} copy-done((f32[64,2,1024]{2,1,0:T(2,128)}, f32[64,2,1024]{2,1,0:T(2,128)S(1)}, u32[]{:S(2)}) %copy-start) | copy-done | bytes 524312
Async XLA Ops:
  49.1 0.8 %copy-start = (f32[64,2,1024]{2,1,0:T(2,128)}, f32[64,2,1024]{2,1,0:T(2,128)S(1)}, u32[]{:S(2)}) copy-start(f32[64,2,1024]{2,1,0:T(2,128)S(1)} %get-tuple-element.712) | copy-start | bytes 1572868

commit v2 on v1

--- a/solution.py
+++ b/solution.py
@@ -21,12 +21,6 @@
 MESH = pl.DeviceIdType.MESH
 F32 = jnp.float32
 BF16 = jnp.bfloat16
-
-
-def from_behind(x, axis, by):
-    count = lax.axis_size(axis)
-    pairs = [(i, i + by) for i in range(count) if 0 <= i + by < count]
-    return lax.ppermute(x, axis, pairs)
 
 
 def bessel_zero(value):
@@ -90,29 +84,28 @@
 
 
 def any_cells(visibilities, cell_offsets, support_index, w_plane, live_counts):
-    own_flat = flatten_groups(
-        visibilities[0], cell_offsets[0], support_index[0], w_plane[0], live_counts[0]
-    )
-    share = G // lax.axis_size("chan")
-    first_row = lax.axis_index("chan") * share
-    owned = lax.psum_scatter(
-        grid_part(own_flat, jnp.int32(0), share * lax.axis_size("chan"), G),
-        "chan",
-        scatter_dimension=0,
-        tiled=True,
-    )
-    low_edge = grid_part(own_flat, -M, M, G)
-    high_edge = grid_part(own_flat, G, M, G)
-    high_sum, low_sum = lax.psum((high_edge, low_edge), "chan")
-    left_in = from_behind(high_sum, "tile", 1)
-    right_in = from_behind(low_sum, "tile", -1)
-    zero_rows = jnp.zeros((share, 2, G), jnp.float32)
-    upper = jnp.concatenate([left_in, zero_rows], axis=0)
-    upper_part = lax.dynamic_slice_in_dim(upper, jnp.minimum(first_row, M), share, 0)
-    lower = jnp.concatenate([zero_rows, right_in], axis=0)
-    lower_start = jnp.clip(first_row - (G - M - share), 0, M)
-    lower_part = lax.dynamic_slice_in_dim(lower, lower_start, share, 0)
-    return owned + upper_part + lower_part
+    tiles, parts = lax.axis_size("tile"), lax.axis_size("chan")
+    share = G // parts
+    first_row = lax.axis_index("chan") * share - M
+    held = jnp.stack(
+        flatten_groups(visibilities[0], cell_offsets[0], support_index[0], w_plane[0], live_counts[0])
+    )
+
+    def step(_, carry):
+        total, held = carry
+        total = total + grid_part(held, first_row, share + 2 * M, G)
+        return total, lax.ppermute(held, "chan", [(i, (i + 1) % parts) for i in range(parts)])
+
+    total, _ = lax.fori_loop(0, parts, step, (jnp.zeros((share + 2 * M, 2, G), F32), held))
+    last = parts - 1
+    left_in = lax.ppermute(
+        total[share + M :], ("tile", "chan"), [(t * parts + last, (t + 1) * parts) for t in range(tiles - 1)]
+    )
+    right_in = lax.ppermute(
+        total[:M], ("tile", "chan"), [(t * parts, (t - 1) * parts + last) for t in range(1, tiles)]
+    )
+    owned = total[M : M + share]
+    return owned.at[:M].add(left_in).at[share - M :].add(right_in)
 
 
 def class_table():
@@ -275,7 +268,7 @@
 
     for i in range(1, nc):
         chan_flag(i, lax.rem(c + i, nc)).wait_recv()
-    flag[...] = jnp.max(chan_flags[...], axis=0)
+    flag[0, 0] = (jnp.max(chan_flags[...]) > 0.5).astype(jnp.int32)
     for i in range(1, nt):
         tile_flag(i, t).wait_send()
     for i in range(1, nc):
@@ -358,10 +351,10 @@
             jax.ShapeDtypeStruct((nc, 4 * GROUPS_IN, FIELDS * LOW), F32),
             jax.ShapeDtypeStruct((nc, 8, FIELDS * LOW), F32),
             jax.ShapeDtypeStruct((128, 128), BF16),
-            jax.ShapeDtypeStruct((8, 128), F32),
+            jax.ShapeDtypeStruct((1, 1), jnp.int32),
         ),
         in_specs=[pl.BlockSpec(memory_space=pl.ANY)] * 4 + [pl.BlockSpec(memory_space=pltpu.SMEM)],
-        out_specs=(vmem,) * 4,
+        out_specs=(vmem, vmem, vmem, pl.BlockSpec(memory_space=pltpu.SMEM)),
         scratch_shapes=[
             pltpu.VMEM((2, slots), F32),
             pltpu.VMEM((2, slots), jnp.int32),
@@ -394,7 +387,7 @@
         )(got, edge, table)
 
     return lax.cond(
-        flag[0, 0] > 0.5, any_cells, usual, visibilities, cell_offsets, support_index, w_plane, live_counts
+        flag[0, 0] > 0, any_cells, usual, visibilities, cell_offsets, support_index, w_plane, live_counts
     )
 
 

time: 57 us -> 41.6 us (0.73)
  the two profiles are of different devices: /device:TPU:1 before, /device:TPU:5 now
where the time goes in v2:
time: 41.6 us; the launch traced here: 41.4 us
  Pallas kernels  40.2 us (97%)
  between operations  1.22 us (3%)
    pallas_call x1, Pallas kernels, usual(): pl.pallas_call(owned_rows, out_shape=jax.ShapeDtypeStruct((G // nc, 2, G)...  23.5 us
    pallas_call x1, Pallas kernels, per_device(): pl.pallas_call(exchange, out_shape=(jax.ShapeDtypeStruct((nc, 4 * GROUPS_...  16.6 us

profile of v2, /device:TPU:5, one launch (start us, length us, event | category | flops | bytes accessed | tf_op | source)
XLA Modules:
  0.0 41.4 jit_solution(17094680062475726845)
XLA Ops:
  0.7 16.6 %shard_map.57 = (f32[16,16,256]{2,1,0:T(8,128)S(1)}, f32[16,8,256]{2,1,0:T(8,128)S(1)}, bf16[128,128]{1,0:T(8,128)(2,1)S(1)}, s32[1,1]{1,0:T(1,128)}) custom-call(f32[1,1,2,2048]{3,2,1,0:T(2,128)} %vis.1, s32[1,1,2,2048]{3,2,1,0:T(2,128)} %cell.1, s32[1,1,2048]{2,1,0:T(1,128)} %sup.1, s32[1,1,2048]{2,1,0:T(1,128)} %wpl.1, s32[1,1]{1,0:T(1,128)S(6)} %copy.27.cnt), custom_call_target="tpu_custom_call" | custom-call | tf_op jit(solution)/shard_map/pallas_call | solution.py:348
  17.9 23.5 %conditional.1 = (f32[64,2,1024]{2,1,0:T(2,128)}) conditional(s32[]{:T(128)} %bitcast.9, (f32[16,16,256]{2,1,0:T(8,128)S(1)}, f32[16,8,256]{2,1,0:T(8,128)S(1)}, bf16[128,128]{1,0:T(8,128)(2,1)S(1)}) %tuple.27, (s32[1,1]{1,0:T(1,128)}, f32[1,1,2,2048]{3,2,1,0:T(2,128)}, s32[1,1,2,2048]{3,2,1,0:T(2,128)}, s32[1,1,2048]{2,1,0:T(1,128)}, ...), branch_computations={%region_0.0_spmd, %region_1.6_spmd} | conditional | flops 334978816 | bytes 18040382 | solution.py:389
  17.9 23.5 %branch_0_fun.1 = f32[64,2,1024]{2,1,0:T(2,128)} custom-call(f32[16,16,256]{2,1,0:T(8,128)S(1)} %get-tuple-element.104.got, f32[16,8,256]{2,1,0:T(8,128)S(1)} %get-tuple-element.105.edge, bf16[128,128]{1,0:T(8,128)(2,1)S(1)} %get-tuple-element.106.table), custom_call_target="tpu_custom_call" | custom-call | tf_op jit(solution)/shard_map/cond/branch_0_fun/pallas_call | solution.py:380

commit v3 on v2

--- a/solution.py
+++ b/solution.py
@@ -109,22 +109,21 @@
 
 
 def class_table():
-    klass = lax.broadcasted_iota(jnp.int32, (128, 128), 0)
-    distance = lax.broadcasted_iota(jnp.int32, (128, 128), 1).astype(F32)
+    shape = (2 * M, 4 * PLANES)
+    klass = lax.broadcasted_iota(jnp.int32, shape, 1)
+    distance = jnp.abs(lax.broadcasted_iota(jnp.int32, shape, 0) - M).astype(F32)
     half = (8 * (klass // PLANES + 1)).astype(F32)
     w_coef = 0.5 * (klass % PLANES + 1).astype(F32) / PLANES
-    ratio = distance / half
-    inside = (ratio < 1.0) & (klass < 4 * PLANES)
-    bound = jnp.minimum(ratio, 1.0)
-    square = bound * bound
+    ratio = jnp.minimum(distance / half, 1.0)
+    square = ratio * ratio
     radius = jnp.sqrt(jnp.maximum(1.0 - square, 0.0))
-    bessel = bessel_zero(BETA * radius) / bessel_zero(jnp.full((128, 128), BETA, F32))
+    bessel = bessel_zero(BETA * radius) / bessel_zero(jnp.full(shape, BETA, F32))
     taper = jnp.cos(jnp.pi * w_coef * square)
-    return jnp.where(inside, bessel * taper, 0.0)
-
-
-def exchange(vis, cell, sup, wpl, cnt, got, edge, table, flag, vis_v, cell_v, sup_v, wpl_v, packed, tile_flags, chan_flags,
-             load_sem, send_sem, recv_sem, edge_send, edge_recv, tf_send, tf_recv, cf_send, cf_recv):
+    return jnp.where(ratio < 1.0, bessel * taper, 0.0).astype(BF16)
+
+
+def exchange(vis, cell, sup, wpl, cnt, got, edge, table, flag, vis_v, cell_v, sup_v, wpl_v, packed, tile_flags,
+             load_sem, send_sem, recv_sem, edge_send, edge_recv, tf_send, tf_recv):
     t, c = lax.axis_index("tile"), lax.axis_index("chan")
     nt, nc = lax.axis_size("tile"), lax.axis_size("chan")
     slots = vis_v.shape[-1]
@@ -179,6 +178,17 @@
     over = (jnp.max(carry, axis=0, keepdims=True) > CAP).astype(F32)
     tile_flags[t] = jnp.broadcast_to(over, (8, 128))
 
+    below, above = (t > 0).astype(jnp.int32), (t < nt - 1).astype(jnp.int32)
+    pl.semaphore_wait(bar, nc - 1 + nt - 1 + below + above)
+
+    def tile_flag(i, slot):
+        return pltpu.make_async_remote_copy(
+            src_ref=tile_flags.at[t], dst_ref=tile_flags.at[slot], send_sem=tf_send.at[i], recv_sem=tf_recv.at[slot],
+            device_id=(lax.rem(t + i, nt), c), device_id_type=MESH)
+
+    for i in range(1, nt):
+        tile_flag(i, t).start()
+
     group = jnp.where(live, (bucket + 1) * GROUPS_IN + rank // LOW, -1)
     place = rank % LOW
     groups = packed.shape[0]
@@ -197,18 +207,11 @@
     spread = jnp.concatenate([jnp.where(at_place, x, 0.0).astype(BF16) for x in pieces], axis=0)
     moved = lax.dot_general(to_group, spread, (((1,), (1,)), ((), ())), preferred_element_type=F32)
     packed[:, 0:128] = moved[:, 0:128] + moved[:, 256:384]
-    packed[:, 128:256] = moved[:, 128:256]
-
-    below, above = (t > 0).astype(jnp.int32), (t < nt - 1).astype(jnp.int32)
-    pl.semaphore_wait(bar, nc - 1 + nt - 1 + below + above)
-
-    def tile_flag(i, slot):
-        return pltpu.make_async_remote_copy(
-            src_ref=tile_flags.at[t], dst_ref=tile_flags.at[slot], send_sem=tf_send.at[i], recv_sem=tf_recv.at[slot],
-            device_id=(lax.rem(t + i, nt), c), device_id_type=MESH)
-
     for i in range(1, nt):
-        tile_flag(i, t).start()
+        tile_flag(i, lax.rem(t + i, nt)).wait_recv()
+    over = jnp.max(tile_flags[...], axis=0)[0:1]
+    spare = lax.broadcasted_iota(jnp.int32, (1, 128), 1) >= 3 * LOW
+    packed[:, 128:256] = moved[:, 128:256] + jnp.where(spare, over, 0.0)
 
     width = 4 * GROUPS_IN
 
@@ -242,19 +245,7 @@
 
     got[c] = packed[pl.ds(pl.multiple_of(8 * c, 8), width), :]
 
-    for i in range(1, nt):
-        tile_flag(i, lax.rem(t + i, nt)).wait_recv()
-    chan_flags[c] = jnp.max(tile_flags[...], axis=0)
-
-    def chan_flag(i, slot):
-        return pltpu.make_async_remote_copy(
-            src_ref=chan_flags.at[c], dst_ref=chan_flags.at[slot], send_sem=cf_send.at[i], recv_sem=cf_recv.at[slot],
-            device_id=(t, lax.rem(c + i, nc)), device_id_type=MESH)
-
-    for i in range(1, nc):
-        chan_flag(i, c).start()
-
-    table[...] = class_table().astype(BF16)
+    table[...] = class_table()
 
     for i in range(1, nc):
         payload(i, lax.rem(c + i, nc)).wait_recv()
@@ -266,14 +257,12 @@
                 src_ref=packed.at[pl.ds(0, GROUPS_IN)], dst_ref=edge.at[g, 0:GROUPS_IN], send_sem=edge_send.at[0],
                 recv_sem=edge_recv.at[g], device_id=(t, g), device_id_type=MESH).wait_recv()
 
-    for i in range(1, nc):
-        chan_flag(i, lax.rem(c + i, nc)).wait_recv()
-    flag[0, 0] = (jnp.max(chan_flags[...]) > 0.5).astype(jnp.int32)
+    top = jnp.max(jnp.max(got[:, :, 128:256], axis=0), axis=0, keepdims=True)
+    flag[0, 0] = (jnp.max(jnp.where(spare, top, 0.0)) > 0.5).astype(jnp.int32)
     for i in range(1, nt):
         tile_flag(i, t).wait_send()
     for i in range(1, nc):
         payload(i, c).wait_send()
-        chan_flag(i, c).wait_send()
 
     @pl.when(t < nt - 1)
     def _():
@@ -284,12 +273,25 @@
         edge_down().wait_send()
 
 
-def owned_rows(got, edge, table, out, rows, total):
+def turned(values, by, sub):
+    for bit in (32, 16, 8):
+        chosen = (by & bit) != 0
+        values = [jnp.where(chosen, values[(k - bit // 8) % 8], values[k]) for k in range(8)]
+    for bit in (4, 2, 1):
+        chosen = (by & bit) != 0
+        rolled = [pltpu.roll(x, bit, 0) for x in values]
+        values = [
+            jnp.where(chosen, jnp.where(sub < bit, rolled[(k - 1) % 8], rolled[k]), values[k]) for k in range(8)
+        ]
+    return values
+
+
+def owned_rows(got, edge, table, out, real, whole, total, weights, columns):
     c = lax.axis_index("chan")
-    nc = got.shape[0]
-    per = got.shape[1]
+    nc, per = got.shape[0], got.shape[1]
     main = nc * per
     count = main + nc * 8
+    quarter = count // 4
 
     lanes = lax.broadcasted_iota(jnp.int32, (1, 256), 1) // LOW
     both = jnp.concatenate([got[...].reshape(main, 256), edge[...].reshape(nc * 8, 256)], axis=0)
@@ -302,42 +304,78 @@
         lax.broadcasted_iota(jnp.int32, (count, count), 0) < lax.broadcasted_iota(jnp.int32, (count, count), 1)
     ).astype(F32).astype(BF16)
     rank = jnp.dot(jnp.broadcast_to(used, (8, count)).astype(BF16), before, preferred_element_type=F32)[0:1]
-    pick = jnp.where(
-        (lax.broadcasted_iota(jnp.int32, (count, count), 0).astype(F32) == rank) & (used > 0.5), 1.0, 0.0
-    ).astype(BF16)
+    rank = jnp.where(used > 0.5, rank, -1.0)
+    place = lax.broadcasted_iota(jnp.int32, (count, count), 0)
+    place = (4 * (place % quarter) + place // quarter).astype(F32)
+    pick = jnp.where(place == rank, 1.0, 0.0).astype(BF16)
     high = both.astype(BF16)
     low = (both - high.astype(F32)).astype(BF16)
-    rows[...] = jnp.dot(pick, high, preferred_element_type=F32) + jnp.dot(pick, low, preferred_element_type=F32)
-    trips = (jnp.sum(used).astype(jnp.int32) + 7) // 8
+    rows = jnp.dot(pick, high, preferred_element_type=F32) + jnp.dot(pick, low, preferred_element_type=F32)
+    spot = lax.broadcasted_iota(jnp.int32, (quarter, 128), 1) // LOW
+
+    def field(f):
+        part, offset = divmod(f, 4)
+        result = None
+        for s in range(4):
+            x = rows[s * quarter : (s + 1) * quarter, 128 * part : 128 * part + 128]
+            if (s - offset) % 4:
+                x = pltpu.roll(x, ((s - offset) % 4) * LOW, 1)
+            result = x if result is None else jnp.where(spot == s, x, result)
+        return result
+
+    real[0], real[1] = field(0), field(1)
+    whole[0], whole[1] = field(2).astype(jnp.int32) - M, field(3).astype(jnp.int32) - M
+    whole[2] = (field(4) * float(PLANES) + field(5)).astype(jnp.int32)
+    size = weights.shape[-1]
+    lines = size // 128
+    chunks = (jnp.sum(used).astype(jnp.int32) + 4 * lines - 1) // (4 * lines)
 
     total[...] = jnp.zeros_like(total)
-    lane = lax.broadcasted_iota(jnp.int32, (256, 128), 1)
-
-    def body(i, carry):
-        block = rows[pl.ds(pl.multiple_of(8 * i, 8), 8), :]
-        klass = block[:, 128 : 128 + LOW] * float(PLANES) + block[:, 128 + LOW : 128 + 2 * LOW]
-        first = block[:, 0:128].T
-        second = jnp.concatenate([klass, block[:, 128 + LOW : 256]], axis=1).T
-
-        def field(x, f):
+    sub = lax.broadcasted_iota(jnp.int32, (8, size), 0)
+
+    def fill(i, slot):
+        def line(ref, f):
             return jnp.concatenate(
-                [jnp.broadcast_to(x[f * LOW : (f + 1) * LOW, r : r + 1], (LOW, 128)) for r in range(8)], axis=0)
-
-        re, im = field(first, 0), field(first, 1)
-        col, row = field(first, 2).astype(jnp.int32), field(first, 3).astype(jnp.int32)
-        hot = (field(second, 0).astype(jnp.int32) == lane).astype(F32).astype(BF16)
-        values = jnp.dot(hot, table[...], preferred_element_type=F32)
-
-        def look_up(distance):
-            return jnp.take_along_axis(values, jnp.minimum(jnp.abs(distance), 127), axis=1, mode="promise_in_bounds")
-
-        weights = (look_up(lane // 2 - row) * jnp.where(lane % 2 == 0, re, im)).astype(BF16)
-        columns = jnp.concatenate([look_up(lane + 128 * b - col).astype(BF16) for b in range(G // 128)], axis=1)
-        total[...] += lax.dot_general(weights, columns, (((0,), (0,)), ((), ())), preferred_element_type=F32)
+                [jnp.broadcast_to(ref[f, pl.ds(lines * i + h, 1), :], (8, 128)) for h in range(lines)], axis=1)
+
+        klass = line(whole, 2)
+        hot = jnp.concatenate([(klass == sub + 8 * k).astype(F32) for k in range(8)], axis=0).astype(BF16)
+        values = jnp.dot(table[...], hot, preferred_element_type=F32)
+        values = [values[8 * k : 8 * k + 8] for k in range(8)]
+        row = line(whole, 1)
+        by, first = row & 63, row >> 6
+        mine = [
+            jnp.where(jnp.where(sub + 8 * k < by, first + 1, first) == 0, x, 0.0)
+            for k, x in enumerate(turned(values, by, sub))
+        ]
+        re, im = line(real, 0), line(real, 1)
+        weights[slot, 0:64] = jnp.concatenate([x * re for x in mine], axis=0).astype(BF16)
+        weights[slot, 64:128] = jnp.concatenate([x * im for x in mine], axis=0).astype(BF16)
+        col = line(whole, 0)
+        by, first = col & 63, col >> 6
+        window = jnp.concatenate(turned(values, by, sub), axis=0).astype(BF16)
+        block = jnp.concatenate(
+            [jnp.where(sub + 8 * k < by, first + 1, first).astype(F32) for k in range(8)], axis=0).astype(BF16)
+        for b in range(G // 64):
+            columns[slot, 64 * b : 64 * b + 64] = jnp.where(
+                block == jnp.asarray(b, BF16), window, jnp.asarray(0, BF16))
+
+    def add(slot):
+        total[...] += lax.dot_general(
+            weights[slot], columns[slot], (((1,), (1,)), ((), ())), preferred_element_type=F32)
+
+    fill(0, 0)
+
+    def body(j, carry):
+        fill(2 * j + 1, 1)
+        add(0)
+        fill(2 * j + 2, 0)
+        add(1)
         return carry
 
-    lax.fori_loop(0, trips, body, 0)
-    out[...] = total[...].reshape(out.shape)
+    lax.fori_loop(0, (chunks + 1) // 2, body, 0)
+    out[:, 0, :] = total[0:64]
+    out[:, 1, :] = total[64:128]
 
 
 def per_device(visibilities, cell_offsets, support_index, w_plane, live_counts):
@@ -350,7 +388,7 @@
         out_shape=(
             jax.ShapeDtypeStruct((nc, 4 * GROUPS_IN, FIELDS * LOW), F32),
             jax.ShapeDtypeStruct((nc, 8, FIELDS * LOW), F32),
-            jax.ShapeDtypeStruct((128, 128), BF16),
+            jax.ShapeDtypeStruct((2 * M, 4 * PLANES), BF16),
             jax.ShapeDtypeStruct((1, 1), jnp.int32),
         ),
         in_specs=[pl.BlockSpec(memory_space=pl.ANY)] * 4 + [pl.BlockSpec(memory_space=pltpu.SMEM)],
@@ -362,7 +400,6 @@
             pltpu.VMEM((1, slots), jnp.int32),
             pltpu.VMEM((groups, FIELDS * LOW), F32),
             pltpu.VMEM((nt, 8, 128), F32),
-            pltpu.VMEM((nc, 8, 128), F32),
             pltpu.SemaphoreType.DMA((4,)),
             pltpu.SemaphoreType.DMA((nc,)),
             pltpu.SemaphoreType.DMA((nc,)),
@@ -370,11 +407,11 @@
             pltpu.SemaphoreType.DMA((nc,)),
             pltpu.SemaphoreType.DMA((nt,)),
             pltpu.SemaphoreType.DMA((nt,)),
-            pltpu.SemaphoreType.DMA((nc,)),
-            pltpu.SemaphoreType.DMA((nc,)),
         ],
         compiler_params=pltpu.CompilerParams(collective_id=0, has_side_effects=True, vmem_limit_bytes=62 << 20),
     )(visibilities, cell_offsets, support_index, w_plane, live_counts)
+
+    groups_got = nc * (4 * GROUPS_IN + 8)
 
     def usual(*_):
         return pl.pallas_call(
@@ -382,7 +419,13 @@
             out_shape=jax.ShapeDtypeStruct((G // nc, 2, G), F32),
             in_specs=[vmem] * 3,
             out_specs=vmem,
-            scratch_shapes=[pltpu.VMEM((nc * (4 * GROUPS_IN + 8), FIELDS * LOW), F32), pltpu.VMEM((2 * G // nc, G), F32)],
+            scratch_shapes=[
+                pltpu.VMEM((2, groups_got // 4, 128), F32),
+                pltpu.VMEM((3, groups_got // 4, 128), jnp.int32),
+                pltpu.VMEM((2 * G // nc, G), F32),
+                pltpu.VMEM((2, 2 * G // nc, 512), BF16),
+                pltpu.VMEM((2, G, 512), BF16),
+            ],
             compiler_params=pltpu.CompilerParams(vmem_limit_bytes=40 << 20),
         )(got, edge, table)
 

time: 41.6 us -> 26.7 us (0.64)
  the two profiles are of different devices: /device:TPU:5 before, /device:TPU:1 now
where the time goes in v3:
time: 26.7 us; the launch traced here: 26.5 us
  Pallas kernels  25.3 us (95%)
  between operations  1.22 us (5%)
    pallas_call x1, Pallas kernels, per_device(): pl.pallas_call(exchange, out_shape=(jax.ShapeDtypeStruct((nc, 4 * GROUPS_...  19.2 us
    pallas_call x1, Pallas kernels, usual(): pl.pallas_call(owned_rows, out_shape=jax.ShapeDtypeStruct((G // nc, 2, G)...  6.1 us

profile of v3, /device:TPU:1, one launch (start us, length us, event | category | flops | bytes accessed | tf_op | source)
XLA Modules:
  0.0 26.5 jit_solution(5061251455602726480)
XLA Ops:
  0.7 19.2 %shard_map.57 = (f32[16,16,256]{2,1,0:T(8,128)S(1)}, f32[16,8,256]{2,1,0:T(8,128)S(1)}, bf16[64,64]{1,0:T(8,128)(2,1)S(1)}, s32[1,1]{1,0:T(1,128)}) custom-call(f32[1,1,2,2048]{3,2,1,0:T(2,128)} %vis.1, s32[1,1,2,2048]{3,2,1,0:T(2,128)} %cell.1, s32[1,1,2048]{2,1,0:T(1,128)} %sup.1, s32[1,1,2048]{2,1,0:T(1,128)} %wpl.1, s32[1,1]{1,0:T(1,128)S(6)} %copy.27.cnt), custom_call_target="tpu_custom_call" | custom-call | tf_op jit(solution)/shard_map/pallas_call | solution.py:386
  20.4 6.1 %conditional.1 = (f32[64,2,1024]{2,1,0:T(2,128)}) conditional(s32[]{:T(128)} %bitcast.9, (f32[16,16,256]{2,1,0:T(8,128)S(1)}, f32[16,8,256]{2,1,0:T(8,128)S(1)}, bf16[64,64]{1,0:T(8,128)(2,1)S(1)}) %tuple.27, (s32[1,1]{1,0:T(1,128)}, f32[1,1,2,2048]{3,2,1,0:T(2,128)}, s32[1,1,2,2048]{3,2,1,0:T(2,128)}, s32[1,1,2048]{2,1,0:T(1,128)}, ...), branch_computations={%region_0.0_spmd, %region_1.6_spmd} | conditional | flops 334978816 | bytes 18040382 | solution.py:432
  20.4 6.1 %branch_0_fun.1 = f32[64,2,1024]{2,1,0:T(2,128)} custom-call(f32[16,16,256]{2,1,0:T(8,128)S(1)} %get-tuple-element.104.got, f32[16,8,256]{2,1,0:T(8,128)S(1)} %get-tuple-element.105.edge, bf16[64,64]{1,0:T(8,128)(2,1)S(1)} %get-tuple-element.106.table), custom_call_target="tpu_custom_call" | custom-call | tf_op jit(solution)/shard_map/cond/branch_0_fun/pallas_call | solution.py:417

commit v4 on v3

--- a/solution.py
+++ b/solution.py
@@ -17,6 +17,7 @@
 CAP = 128
 LOW = 32
 GROUPS_IN = CAP // LOW
+EARLY = 2
 FIELDS = 8
 MESH = pl.DeviceIdType.MESH
 F32 = jnp.float32
@@ -122,8 +123,47 @@
     return jnp.where(ratio < 1.0, bessel * taper, 0.0).astype(BF16)
 
 
-def exchange(vis, cell, sup, wpl, cnt, got, edge, table, flag, vis_v, cell_v, sup_v, wpl_v, packed, tile_flags,
-             load_sem, send_sem, recv_sem, edge_send, edge_recv, tf_send, tf_recv):
+def turned(values, by, sub):
+    for bit in (32, 16, 8):
+        chosen = (by & bit) != 0
+        values = [jnp.where(chosen, values[(k - bit // 8) % 8], values[k]) for k in range(8)]
+    for bit in (4, 2, 1):
+        chosen = (by & bit) != 0
+        rolled = [pltpu.roll(x, bit, 0) for x in values]
+        values = [
+            jnp.where(chosen, jnp.where(sub < bit, rolled[(k - 1) % 8], rolled[k]), values[k]) for k in range(8)
+        ]
+    return values
+
+
+def lay(klass, row, col, re, im, table, weights, columns):
+    sub = lax.broadcasted_iota(jnp.int32, klass.shape, 0)
+    hot = jnp.concatenate([(klass == sub + 8 * k).astype(F32) for k in range(8)], axis=0).astype(BF16)
+    values = jnp.dot(table[...], hot, preferred_element_type=F32)
+    values = [values[8 * k : 8 * k + 8] for k in range(8)]
+    by, first = row & 63, row >> 6
+    mine = [
+        jnp.where(jnp.where(sub + 8 * k < by, first + 1, first) == 0, x, 0.0)
+        for k, x in enumerate(turned(values, by, sub))
+    ]
+    weights[0:64] = jnp.concatenate([x * re for x in mine], axis=0).astype(BF16)
+    weights[64:128] = jnp.concatenate([x * im for x in mine], axis=0).astype(BF16)
+    by, first = col & 63, col >> 6
+    window = jnp.concatenate(turned(values, by, sub), axis=0).astype(BF16)
+    block = jnp.concatenate(
+        [jnp.where(sub + 8 * k < by, first + 1, first).astype(F32) for k in range(8)], axis=0).astype(BF16)
+    for b in range(G // 64):
+        columns[64 * b : 64 * b + 64] = jnp.where(block == jnp.asarray(b, BF16), window, jnp.asarray(0, BF16))
+
+
+def add(total, weights, columns):
+    total[...] += lax.dot_general(
+        weights[...], columns[...], (((1,), (1,)), ((), ())), preferred_element_type=F32)
+
+
+def exchange(vis, cell, sup, wpl, cnt, got, edge, table, total, flag, vis_v, cell_v, sup_v, wpl_v, packed, tile_flags, chan_flags,
+             weights, columns,
+             load_sem, send_sem, recv_sem, edge_send, edge_recv, tf_send, tf_recv, cf_send, cf_recv):
     t, c = lax.axis_index("tile"), lax.axis_index("chan")
     nt, nc = lax.axis_size("tile"), lax.axis_size("chan")
     slots = vis_v.shape[-1]
@@ -176,7 +216,7 @@
         carry = carry + jnp.sum(piece, axis=1, keepdims=True)
     rank = jnp.concatenate(parts, axis=1).astype(jnp.int32)
     over = (jnp.max(carry, axis=0, keepdims=True) > CAP).astype(F32)
-    tile_flags[t] = jnp.broadcast_to(over, (8, 128))
+    tile_flags[t] = jnp.broadcast_to(over, (1, 128))
 
     below, above = (t > 0).astype(jnp.int32), (t < nt - 1).astype(jnp.int32)
     pl.semaphore_wait(bar, nc - 1 + nt - 1 + below + above)
@@ -207,11 +247,7 @@
     spread = jnp.concatenate([jnp.where(at_place, x, 0.0).astype(BF16) for x in pieces], axis=0)
     moved = lax.dot_general(to_group, spread, (((1,), (1,)), ((), ())), preferred_element_type=F32)
     packed[:, 0:128] = moved[:, 0:128] + moved[:, 256:384]
-    for i in range(1, nt):
-        tile_flag(i, lax.rem(t + i, nt)).wait_recv()
-    over = jnp.max(tile_flags[...], axis=0)[0:1]
-    spare = lax.broadcasted_iota(jnp.int32, (1, 128), 1) >= 3 * LOW
-    packed[:, 128:256] = moved[:, 128:256] + jnp.where(spare, over, 0.0)
+    packed[:, 128:256] = moved[:, 128:256]
 
     width = 4 * GROUPS_IN
 
@@ -245,10 +281,81 @@
 
     got[c] = packed[pl.ds(pl.multiple_of(8 * c, 8), width), :]
 
+    for i in range(1, nt):
+        tile_flag(i, lax.rem(t + i, nt)).wait_recv()
+    chan_flags[c] = jnp.max(tile_flags[...], axis=0)
+
+    def chan_flag(i, slot):
+        return pltpu.make_async_remote_copy(
+            src_ref=chan_flags.at[c], dst_ref=chan_flags.at[slot], send_sem=cf_send.at[i], recv_sem=cf_recv.at[slot],
+            device_id=(t, lax.rem(c + i, nc)), device_id_type=MESH)
+
+    for i in order:
+        chan_flag(i, c).start()
+
     table[...] = class_table()
-
-    for i in range(1, nc):
-        payload(i, lax.rem(c + i, nc)).wait_recv()
+    total[...] = jnp.zeros_like(total)
+
+    spot = lax.broadcasted_iota(jnp.int32, (8, 128), 1) // LOW
+    lift = BUCKET * (lax.broadcasted_iota(jnp.int32, (width, 128), 0) // GROUPS_IN - 1) - M
+    row_lanes = lax.broadcasted_iota(jnp.int32, (width, 128), 1) // LOW == 3
+
+    def fields(source):
+        first, second = got[source, :, 0:128], got[source, :, 128:256]
+        cells = first.astype(jnp.int32)
+        cells = jnp.where(row_lanes, cells + lift, cells - M)
+        klass = (second * float(PLANES) + pltpu.roll(second, 3 * LOW, 1)).astype(jnp.int32)
+
+        def lines(x, offset):
+            shifted = [pltpu.roll(x, ((b - offset) % 4) * LOW, 1) if (b - offset) % 4 else x for b in range(4)]
+            made = []
+            for g in range(EARLY):
+                parts = [jnp.broadcast_to(shifted[b][GROUPS_IN * b + g : GROUPS_IN * b + g + 1], (8, 128)) for b in range(4)]
+                line = parts[0]
+                for b in range(1, 4):
+                    line = jnp.where(spot == b, parts[b], line)
+                made.append(line)
+            return made
+
+        return lines(klass, 0), lines(cells, 3), lines(cells, 2), lines(first, 0), lines(first, 1)
+
+    here = 2 * (c // 2)
+
+    def chip(k):
+        q = k % 4
+        dz = q + jnp.where(q == 2, 1, 0) - jnp.where(q == 3, 1, 0)
+        z, y = (here // 2) % 4, here // 8
+        return (((y + k // 4) % 2) * 4 + (z + dz) % 4) * 2
+
+    def prepare(source, slot):
+        both = [a + b for a, b in zip(fields(source), fields(source + 1))]
+        lay(*[jnp.concatenate(x, axis=1) for x in both], table, weights.at[slot], columns.at[slot])
+
+    def arrive(source):
+        pltpu.make_async_remote_copy(
+            src_ref=packed.at[pl.ds(0, width)], dst_ref=got.at[source], send_sem=send_sem.at[1],
+            recv_sem=recv_sem.at[source], device_id=(t, source), device_id_type=MESH).wait_recv()
+
+    arrive(here + (c + 1) % 2)
+    prepare(here, 0)
+
+    def two_chips(j, carry):
+        for odd in (1, 0):
+            source = chip(2 * j + 2 - odd)
+            arrive(source)
+            arrive(source + 1)
+            prepare(source, odd)
+            add(total, weights.at[1 - odd], columns.at[1 - odd])
+        return carry
+
+    chips = nc // 2
+    lax.fori_loop(0, chips // 2 - 1, two_chips, 0)
+    source = chip(chips - 1)
+    arrive(source)
+    arrive(source + 1)
+    prepare(source, 1)
+    add(total, weights.at[0], columns.at[0])
+    add(total, weights.at[1], columns.at[1])
 
     @pl.when(from_low | from_high)
     def _():
@@ -257,12 +364,14 @@
                 src_ref=packed.at[pl.ds(0, GROUPS_IN)], dst_ref=edge.at[g, 0:GROUPS_IN], send_sem=edge_send.at[0],
                 recv_sem=edge_recv.at[g], device_id=(t, g), device_id_type=MESH).wait_recv()
 
-    top = jnp.max(jnp.max(got[:, :, 128:256], axis=0), axis=0, keepdims=True)
-    flag[0, 0] = (jnp.max(jnp.where(spare, top, 0.0)) > 0.5).astype(jnp.int32)
+    for i in range(1, nc):
+        chan_flag(i, lax.rem(c + i, nc)).wait_recv()
+    flag[0, 0] = (jnp.max(jnp.max(chan_flags[...], axis=0)) > 0.5).astype(jnp.int32)
     for i in range(1, nt):
         tile_flag(i, t).wait_send()
     for i in range(1, nc):
         payload(i, c).wait_send()
+        chan_flag(i, c).wait_send()
 
     @pl.when(t < nt - 1)
     def _():
@@ -273,20 +382,7 @@
         edge_down().wait_send()
 
 
-def turned(values, by, sub):
-    for bit in (32, 16, 8):
-        chosen = (by & bit) != 0
-        values = [jnp.where(chosen, values[(k - bit // 8) % 8], values[k]) for k in range(8)]
-    for bit in (4, 2, 1):
-        chosen = (by & bit) != 0
-        rolled = [pltpu.roll(x, bit, 0) for x in values]
-        values = [
-            jnp.where(chosen, jnp.where(sub < bit, rolled[(k - 1) % 8], rolled[k]), values[k]) for k in range(8)
-        ]
-    return values
-
-
-def owned_rows(got, edge, table, out, real, whole, total, weights, columns):
+def owned_rows(got, edge, table, begun, out, real, whole, total, weights, columns):
     c = lax.axis_index("chan")
     nc, per = got.shape[0], got.shape[1]
     main = nc * per
@@ -300,6 +396,8 @@
     both = both + jnp.where(lanes == 3, shift, 0).astype(F32)
     used = jnp.where(lax.broadcasted_iota(jnp.int32, (128, count), 0) == 6 * LOW - 128, both[:, 128:256].T, 0.0)
     used = jnp.sum(used, axis=0, keepdims=True)
+    at = lax.broadcasted_iota(jnp.int32, (1, count), 1)
+    used = jnp.where((at < main) & (at % GROUPS_IN < EARLY), 0.0, used)
     before = (
         lax.broadcasted_iota(jnp.int32, (count, count), 0) < lax.broadcasted_iota(jnp.int32, (count, count), 1)
     ).astype(F32).astype(BF16)
@@ -330,47 +428,23 @@
     lines = size // 128
     chunks = (jnp.sum(used).astype(jnp.int32) + 4 * lines - 1) // (4 * lines)
 
-    total[...] = jnp.zeros_like(total)
-    sub = lax.broadcasted_iota(jnp.int32, (8, size), 0)
+    total[...] = begun[...]
 
     def fill(i, slot):
         def line(ref, f):
             return jnp.concatenate(
                 [jnp.broadcast_to(ref[f, pl.ds(lines * i + h, 1), :], (8, 128)) for h in range(lines)], axis=1)
 
-        klass = line(whole, 2)
-        hot = jnp.concatenate([(klass == sub + 8 * k).astype(F32) for k in range(8)], axis=0).astype(BF16)
-        values = jnp.dot(table[...], hot, preferred_element_type=F32)
-        values = [values[8 * k : 8 * k + 8] for k in range(8)]
-        row = line(whole, 1)
-        by, first = row & 63, row >> 6
-        mine = [
-            jnp.where(jnp.where(sub + 8 * k < by, first + 1, first) == 0, x, 0.0)
-            for k, x in enumerate(turned(values, by, sub))
-        ]
-        re, im = line(real, 0), line(real, 1)
-        weights[slot, 0:64] = jnp.concatenate([x * re for x in mine], axis=0).astype(BF16)
-        weights[slot, 64:128] = jnp.concatenate([x * im for x in mine], axis=0).astype(BF16)
-        col = line(whole, 0)
-        by, first = col & 63, col >> 6
-        window = jnp.concatenate(turned(values, by, sub), axis=0).astype(BF16)
-        block = jnp.concatenate(
-            [jnp.where(sub + 8 * k < by, first + 1, first).astype(F32) for k in range(8)], axis=0).astype(BF16)
-        for b in range(G // 64):
-            columns[slot, 64 * b : 64 * b + 64] = jnp.where(
-                block == jnp.asarray(b, BF16), window, jnp.asarray(0, BF16))
-
-    def add(slot):
-        total[...] += lax.dot_general(
-            weights[slot], columns[slot], (((1,), (1,)), ((), ())), preferred_element_type=F32)
+        lay(line(whole, 2), line(whole, 1), line(whole, 0), line(real, 0), line(real, 1), table,
+            weights.at[slot], columns.at[slot])
 
     fill(0, 0)
 
     def body(j, carry):
         fill(2 * j + 1, 1)
-        add(0)
+        add(total, weights.at[0], columns.at[0])
         fill(2 * j + 2, 0)
-        add(1)
+        add(total, weights.at[1], columns.at[1])
         return carry
 
     lax.fori_loop(0, (chunks + 1) // 2, body, 0)
@@ -383,23 +457,27 @@
     slots = visibilities.shape[-1]
     groups = (G // BUCKET + 2) * GROUPS_IN
     vmem = pl.BlockSpec(memory_space=pltpu.VMEM)
-    got, edge, table, flag = pl.pallas_call(
+    got, edge, table, begun, flag = pl.pallas_call(
         exchange,
         out_shape=(
             jax.ShapeDtypeStruct((nc, 4 * GROUPS_IN, FIELDS * LOW), F32),
             jax.ShapeDtypeStruct((nc, 8, FIELDS * LOW), F32),
             jax.ShapeDtypeStruct((2 * M, 4 * PLANES), BF16),
+            jax.ShapeDtypeStruct((2 * G // nc, G), F32),
             jax.ShapeDtypeStruct((1, 1), jnp.int32),
         ),
         in_specs=[pl.BlockSpec(memory_space=pl.ANY)] * 4 + [pl.BlockSpec(memory_space=pltpu.SMEM)],
-        out_specs=(vmem, vmem, vmem, pl.BlockSpec(memory_space=pltpu.SMEM)),
+        out_specs=(vmem, vmem, vmem, vmem, pl.BlockSpec(memory_space=pltpu.SMEM)),
         scratch_shapes=[
             pltpu.VMEM((2, slots), F32),
             pltpu.VMEM((2, slots), jnp.int32),
             pltpu.VMEM((1, slots), jnp.int32),
             pltpu.VMEM((1, slots), jnp.int32),
             pltpu.VMEM((groups, FIELDS * LOW), F32),
-            pltpu.VMEM((nt, 8, 128), F32),
+            pltpu.VMEM((nt, 1, 128), F32),
+            pltpu.VMEM((nc, 1, 128), F32),
+            pltpu.VMEM((2, 2 * G // nc, 512), BF16),
+            pltpu.VMEM((2, G, 512), BF16),
             pltpu.SemaphoreType.DMA((4,)),
             pltpu.SemaphoreType.DMA((nc,)),
             pltpu.SemaphoreType.DMA((nc,)),
@@ -407,6 +485,8 @@
             pltpu.SemaphoreType.DMA((nc,)),
             pltpu.SemaphoreType.DMA((nt,)),
             pltpu.SemaphoreType.DMA((nt,)),
+            pltpu.SemaphoreType.DMA((nc,)),
+            pltpu.SemaphoreType.DMA((nc,)),
         ],
         compiler_params=pltpu.CompilerParams(collective_id=0, has_side_effects=True, vmem_limit_bytes=62 << 20),
     )(visibilities, cell_offsets, support_index, w_plane, live_counts)
@@ -417,7 +497,7 @@
         return pl.pallas_call(
             owned_rows,
             out_shape=jax.ShapeDtypeStruct((G // nc, 2, G), F32),
-            in_specs=[vmem] * 3,
+            in_specs=[vmem] * 4,
             out_specs=vmem,
             scratch_shapes=[
                 pltpu.VMEM((2, groups_got // 4, 128), F32),
@@ -427,7 +507,7 @@
                 pltpu.VMEM((2, G, 512), BF16),
             ],
             compiler_params=pltpu.CompilerParams(vmem_limit_bytes=40 << 20),
-        )(got, edge, table)
+        )(got, edge, table, begun)
 
     return lax.cond(
         flag[0, 0] > 0, any_cells, usual, visibilities, cell_offsets, support_index, w_plane, live_counts

time: 26.7 us -> 25.2 us (0.944)
  the two profiles are of different devices: /device:TPU:1 before, /device:TPU:8 now
where the time goes in v4:
time: 25.2 us; the launch traced here: 25 us
  Pallas kernels  23.8 us (94%)
  between operations  1.22 us (5%)
    pallas_call x1, Pallas kernels, per_device(): pl.pallas_call(exchange, out_shape=(jax.ShapeDtypeStruct((nc, 4 * GROUPS_...  19.7 us
    pallas_call x1, Pallas kernels, usual(): pl.pallas_call(owned_rows, out_shape=jax.ShapeDtypeStruct((G // nc, 2, G)...  4.06 us

profile of v4, /device:TPU:8, one launch (start us, length us, event | category | flops | bytes accessed | tf_op | source)
XLA Modules:
  0.0 25.0 jit_solution(2941687074507006939)
XLA Ops:
  0.7 19.7 %shard_map.57 = (f32[16,16,256]{2,1,0:T(8,128)S(1)}, f32[16,8,256]{2,1,0:T(8,128)S(1)}, bf16[64,64]{1,0:T(8,128)(2,1)S(1)}, f32[128,1024]{1,0:T(8,128)S(1)}, s32[1,1]{1,0:T(1,128)}) custom-call(f32[1,1,2,2048]{3,2,1,0:T(2,128)} %vis.1, s32[1,1,2,2048]{3,2,1,0:T(2,128)} %cell.1, s32[1,1,2048]{2,1,0:T(1,128)} %sup.1, s32[1,1,2048]{2,1,0:T(1,128)} %wpl.1, ...), custom_call_target="tpu_custom_call" | custom-call | tf_op jit(solution)/shard_map/pallas_call | solution.py:460
  20.9 4.1 %conditional.1 = (f32[64,2,1024]{2,1,0:T(2,128)}) conditional(s32[]{:T(128)} %bitcast.9, (f32[16,16,256]{2,1,0:T(8,128)S(1)}, f32[16,8,256]{2,1,0:T(8,128)S(1)}, bf16[64,64]{1,0:T(8,128)(2,1)S(1)}, f32[128,1024]{1,0:T(8,128)S(1)}) %tuple.27, (s32[1,1]{1,0:T(1,128)}, f32[1,1,2,2048]{3,2,1,0:T(2,128)}, s32[1,1,2,2048]{3,2,1,0:T(2,128)}, ...), branch_computations={%region_0.0_spmd, %region_1.6_spmd} | conditional | flops 334978816 | bytes 18040382 | solution.py:512
  21.0 4.1 %branch_0_fun.1 = f32[64,2,1024]{2,1,0:T(2,128)} custom-call(f32[16,16,256]{2,1,0:T(8,128)S(1)} %get-tuple-element.106.got, f32[16,8,256]{2,1,0:T(8,128)S(1)} %get-tuple-element.107.edge, bf16[64,64]{1,0:T(8,128)(2,1)S(1)} %get-tuple-element.108.table, f32[128,1024]{1,0:T(8,128)S(1)} %get-tuple-element.109.begun), custom_call_target="tpu_custom_call" | custom-call | tf_op jit(solution)/shard_map/cond/branch_0_fun/pallas_call | solution.py:497

commit v5 on v4

--- a/solution.py
+++ b/solution.py
@@ -17,7 +17,8 @@
 CAP = 128
 LOW = 32
 GROUPS_IN = CAP // LOW
-EARLY = 2
+EARLY = (0, GROUPS_IN - 1)
+SPAN = 9
 FIELDS = 8
 MESH = pl.DeviceIdType.MESH
 F32 = jnp.float32
@@ -136,7 +137,7 @@
     return values
 
 
-def lay(klass, row, col, re, im, table, weights, columns):
+def lay(klass, row, col, re, im, table, weights, columns, start=0):
     sub = lax.broadcasted_iota(jnp.int32, klass.shape, 0)
     hot = jnp.concatenate([(klass == sub + 8 * k).astype(F32) for k in range(8)], axis=0).astype(BF16)
     values = jnp.dot(table[...], hot, preferred_element_type=F32)
@@ -152,13 +153,14 @@
     window = jnp.concatenate(turned(values, by, sub), axis=0).astype(BF16)
     block = jnp.concatenate(
         [jnp.where(sub + 8 * k < by, first + 1, first).astype(F32) for k in range(8)], axis=0).astype(BF16)
-    for b in range(G // 64):
-        columns[64 * b : 64 * b + 64] = jnp.where(block == jnp.asarray(b, BF16), window, jnp.asarray(0, BF16))
-
-
-def add(total, weights, columns):
-    total[...] += lax.dot_general(
-        weights[...], columns[...], (((1,), (1,)), ((), ())), preferred_element_type=F32)
+    for b in range(columns.shape[0] // 64):
+        columns[64 * b : 64 * b + 64] = jnp.where(block == jnp.asarray(start + b, BF16), window, jnp.asarray(0, BF16))
+
+
+def add(total, weights, columns, start=0):
+    stop = 64 * start + columns.shape[0]
+    total[64 * start : stop] += lax.dot_general(
+        columns[...], weights[...], (((1,), (1,)), ((), ())), preferred_element_type=F32)
 
 
 def exchange(vis, cell, sup, wpl, cnt, got, edge, table, total, flag, vis_v, cell_v, sup_v, wpl_v, packed, tile_flags, chan_flags,
@@ -200,22 +202,26 @@
 
     live = lax.broadcasted_iota(jnp.int32, (1, slots), 1) < cnt[0, 0]
     row = cell_v[0:1]
-    bucket = jnp.where(live, row // BUCKET, -1)
     buckets = G // BUCKET
-    hot = (lax.broadcasted_iota(jnp.int32, (buckets, slots), 0) == bucket).astype(F32)
+    bucket = row // BUCKET
+    right = cell_v[1:2] >= G // 2
+    side = jnp.where(live, bucket + jnp.where(right, buckets, 0), -1)
+    hot = (lax.broadcasted_iota(jnp.int32, (2 * buckets, slots), 0) == side).astype(F32)
     step = 256
     before = (
         lax.broadcasted_iota(jnp.int32, (step, step), 0) < lax.broadcasted_iota(jnp.int32, (step, step), 1)
     ).astype(F32).astype(BF16)
     parts = []
-    carry = jnp.zeros((buckets, 1), F32)
+    carry = jnp.zeros((2 * buckets, 1), F32)
     for s in range(0, slots, step):
         piece = hot[:, s : s + step]
         ahead = jnp.dot(piece.astype(BF16), before, preferred_element_type=F32) + carry
         parts.append(jnp.sum(piece * ahead, axis=0, keepdims=True))
         carry = carry + jnp.sum(piece, axis=1, keepdims=True)
     rank = jnp.concatenate(parts, axis=1).astype(jnp.int32)
-    over = (jnp.max(carry, axis=0, keepdims=True) > CAP).astype(F32)
+    full = jnp.max(carry[:buckets] + carry[buckets:], axis=0, keepdims=True) > CAP
+    full = full | (jnp.max(carry, axis=0, keepdims=True) > CAP - LOW)
+    over = full.astype(F32)
     tile_flags[t] = jnp.broadcast_to(over, (1, 128))
 
     below, above = (t > 0).astype(jnp.int32), (t < nt - 1).astype(jnp.int32)
@@ -229,8 +235,9 @@
     for i in range(1, nt):
         tile_flag(i, t).start()
 
-    group = jnp.where(live, (bucket + 1) * GROUPS_IN + rank // LOW, -1)
-    place = rank % LOW
+    spot = jnp.where(right, CAP - 1 - rank, rank)
+    group = jnp.where(live, (bucket + 1) * GROUPS_IN + (spot >> (LOW.bit_length() - 1)), -1)
+    place = spot & (LOW - 1)
     groups = packed.shape[0]
     to_group = (lax.broadcasted_iota(jnp.int32, (groups, slots), 0) == group).astype(F32).astype(BF16)
     at_place = lax.broadcasted_iota(jnp.int32, (LOW, slots), 0) == place
@@ -297,20 +304,18 @@
     total[...] = jnp.zeros_like(total)
 
     spot = lax.broadcasted_iota(jnp.int32, (8, 128), 1) // LOW
-    lift = BUCKET * (lax.broadcasted_iota(jnp.int32, (width, 128), 0) // GROUPS_IN - 1) - M
-    row_lanes = lax.broadcasted_iota(jnp.int32, (width, 128), 1) // LOW == 3
-
-    def fields(source):
-        first, second = got[source, :, 0:128], got[source, :, 128:256]
-        cells = first.astype(jnp.int32)
-        cells = jnp.where(row_lanes, cells + lift, cells - M)
+
+    def fields(first, second, lift, picks):
+        row_lanes = lax.broadcasted_iota(jnp.int32, first.shape, 1) // LOW == 3
+        cells = first.astype(jnp.int32) - M
+        cells = jnp.where(row_lanes, cells + lift, cells)
         klass = (second * float(PLANES) + pltpu.roll(second, 3 * LOW, 1)).astype(jnp.int32)
 
         def lines(x, offset):
             shifted = [pltpu.roll(x, ((b - offset) % 4) * LOW, 1) if (b - offset) % 4 else x for b in range(4)]
             made = []
-            for g in range(EARLY):
-                parts = [jnp.broadcast_to(shifted[b][GROUPS_IN * b + g : GROUPS_IN * b + g + 1], (8, 128)) for b in range(4)]
+            for pick in picks:
+                parts = [jnp.broadcast_to(shifted[b][r : r + 1], (8, 128)) for b, r in enumerate(pick)]
                 line = parts[0]
                 for b in range(1, 4):
                     line = jnp.where(spot == b, parts[b], line)
@@ -319,6 +324,9 @@
 
         return lines(klass, 0), lines(cells, 3), lines(cells, 2), lines(first, 0), lines(first, 1)
 
+    halves_at = (0, G // 64 - SPAN)
+    lift = BUCKET * (lax.broadcasted_iota(jnp.int32, (width, 128), 0) // GROUPS_IN - 1)
+
     here = 2 * (c // 2)
 
     def chip(k):
@@ -328,8 +336,17 @@
         return (((y + k // 4) % 2) * 4 + (z + dz) % 4) * 2
 
     def prepare(source, slot):
-        both = [a + b for a, b in zip(fields(source), fields(source + 1))]
-        lay(*[jnp.concatenate(x, axis=1) for x in both], table, weights.at[slot], columns.at[slot])
+        made = [
+            fields(got[x, :, 0:128], got[x, :, 128:256], lift, [[GROUPS_IN * b + g for b in range(4)] for g in EARLY])
+            for x in (source, source + 1)
+        ]
+        for h in range(2):
+            lay(*[jnp.concatenate([x[h], y[h]], axis=1) for x, y in zip(*made)], table, weights.at[slot, h],
+                columns.at[slot, h], halves_at[h])
+
+    def add_both(slot):
+        for h in range(2):
+            add(total, weights.at[slot, h], columns.at[slot, h], halves_at[h])
 
     def arrive(source):
         pltpu.make_async_remote_copy(
@@ -345,7 +362,7 @@
             arrive(source)
             arrive(source + 1)
             prepare(source, odd)
-            add(total, weights.at[1 - odd], columns.at[1 - odd])
+            add_both(1 - odd)
         return carry
 
     chips = nc // 2
@@ -354,8 +371,8 @@
     arrive(source)
     arrive(source + 1)
     prepare(source, 1)
-    add(total, weights.at[0], columns.at[0])
-    add(total, weights.at[1], columns.at[1])
+    add_both(0)
+    add_both(1)
 
     @pl.when(from_low | from_high)
     def _():
@@ -363,6 +380,16 @@
             pltpu.make_async_remote_copy(
                 src_ref=packed.at[pl.ds(0, GROUPS_IN)], dst_ref=edge.at[g, 0:GROUPS_IN], send_sem=edge_send.at[0],
                 recv_sem=edge_recv.at[g], device_id=(t, g), device_id_type=MESH).wait_recv()
+        rows = edge[...].reshape(nc * 8, 256)
+        lines = nc // 4
+        picks = [[8 * (4 * n + b) + g for b in range(4)] for g in EARLY for n in range(lines)]
+        made = fields(rows[:, 0:128], rows[:, 128:256], jnp.where(from_low, -BUCKET, 2 * BUCKET), picks)
+        for h in range(2):
+            for n in range(0, lines, 2):
+                lay(*[jnp.concatenate(x[h * lines + n : h * lines + n + 2], axis=1) for x in made], table,
+                    weights.at[n // 2, h], columns.at[n // 2, h], halves_at[h])
+        for n in range(lines // 2):
+            add_both(n)
 
     for i in range(1, nc):
         chan_flag(i, lax.rem(c + i, nc)).wait_recv()
@@ -387,23 +414,23 @@
     nc, per = got.shape[0], got.shape[1]
     main = nc * per
     count = main + nc * 8
-    quarter = count // 4
+    left = nc * (per // GROUPS_IN + 1) * (GROUPS_IN - len(EARLY))
+    quarter = left // 4
 
     lanes = lax.broadcasted_iota(jnp.int32, (1, 256), 1) // LOW
     both = jnp.concatenate([got[...].reshape(main, 256), edge[...].reshape(nc * 8, 256)], axis=0)
     index = lax.broadcasted_iota(jnp.int32, (count, 256), 0)
     shift = jnp.where(index < main, BUCKET * ((index % per) // GROUPS_IN - 1), jnp.where(c == 0, -BUCKET, 2 * BUCKET))
     both = both + jnp.where(lanes == 3, shift, 0).astype(F32)
-    used = jnp.where(lax.broadcasted_iota(jnp.int32, (128, count), 0) == 6 * LOW - 128, both[:, 128:256].T, 0.0)
-    used = jnp.sum(used, axis=0, keepdims=True)
-    at = lax.broadcasted_iota(jnp.int32, (1, count), 1)
-    used = jnp.where((at < main) & (at % GROUPS_IN < EARLY), 0.0, used)
+    used = jnp.max(both[:, 128:256].T[2 * LOW : 3 * LOW], axis=0, keepdims=True)
+    at = lax.broadcasted_iota(jnp.int32, (1, count), 1) % GROUPS_IN
+    used = jnp.where((at == EARLY[0]) | (at == EARLY[1]), 0.0, used)
     before = (
         lax.broadcasted_iota(jnp.int32, (count, count), 0) < lax.broadcasted_iota(jnp.int32, (count, count), 1)
     ).astype(F32).astype(BF16)
     rank = jnp.dot(jnp.broadcast_to(used, (8, count)).astype(BF16), before, preferred_element_type=F32)[0:1]
     rank = jnp.where(used > 0.5, rank, -1.0)
-    place = lax.broadcasted_iota(jnp.int32, (count, count), 0)
+    place = lax.broadcasted_iota(jnp.int32, (left, count), 0)
     place = (4 * (place % quarter) + place // quarter).astype(F32)
     pick = jnp.where(place == rank, 1.0, 0.0).astype(BF16)
     high = both.astype(BF16)
@@ -430,26 +457,19 @@
 
     total[...] = begun[...]
 
-    def fill(i, slot):
+    def body(i, carry):
         def line(ref, f):
             return jnp.concatenate(
                 [jnp.broadcast_to(ref[f, pl.ds(lines * i + h, 1), :], (8, 128)) for h in range(lines)], axis=1)
 
-        lay(line(whole, 2), line(whole, 1), line(whole, 0), line(real, 0), line(real, 1), table,
-            weights.at[slot], columns.at[slot])
-
-    fill(0, 0)
-
-    def body(j, carry):
-        fill(2 * j + 1, 1)
-        add(total, weights.at[0], columns.at[0])
-        fill(2 * j + 2, 0)
-        add(total, weights.at[1], columns.at[1])
+        lay(line(whole, 2), line(whole, 1), line(whole, 0), line(real, 0), line(real, 1), table, weights, columns)
+        add(total, weights, columns)
         return carry
 
-    lax.fori_loop(0, (chunks + 1) // 2, body, 0)
-    out[:, 0, :] = total[0:64]
-    out[:, 1, :] = total[64:128]
+    lax.fori_loop(0, chunks, body, 0)
+    rows = total[...].T
+    out[:, 0, :] = rows[0:64]
+    out[:, 1, :] = rows[64:128]
 
 
 def per_device(visibilities, cell_offsets, support_index, w_plane, live_counts):
@@ -463,7 +483,7 @@
             jax.ShapeDtypeStruct((nc, 4 * GROUPS_IN, FIELDS * LOW), F32),
             jax.ShapeDtypeStruct((nc, 8, FIELDS * LOW), F32),
             jax.ShapeDtypeStruct((2 * M, 4 * PLANES), BF16),
-            jax.ShapeDtypeStruct((2 * G // nc, G), F32),
+            jax.ShapeDtypeStruct((G, 2 * G // nc), F32),
             jax.ShapeDtypeStruct((1, 1), jnp.int32),
         ),
         in_specs=[pl.BlockSpec(memory_space=pl.ANY)] * 4 + [pl.BlockSpec(memory_space=pltpu.SMEM)],
@@ -476,8 +496,8 @@
             pltpu.VMEM((groups, FIELDS * LOW), F32),
             pltpu.VMEM((nt, 1, 128), F32),
             pltpu.VMEM((nc, 1, 128), F32),
-            pltpu.VMEM((2, 2 * G // nc, 512), BF16),
-            pltpu.VMEM((2, G, 512), BF16),
+            pltpu.VMEM((2, 2, 2 * G // nc, 256), BF16),
+            pltpu.VMEM((2, 2, 64 * SPAN, 256), BF16),
             pltpu.SemaphoreType.DMA((4,)),
             pltpu.SemaphoreType.DMA((nc,)),
             pltpu.SemaphoreType.DMA((nc,)),
@@ -491,7 +511,7 @@
         compiler_params=pltpu.CompilerParams(collective_id=0, has_side_effects=True, vmem_limit_bytes=62 << 20),
     )(visibilities, cell_offsets, support_index, w_plane, live_counts)
 
-    groups_got = nc * (4 * GROUPS_IN + 8)
+    groups_left = nc * 5 * (GROUPS_IN - len(EARLY))
 
     def usual(*_):
         return pl.pallas_call(
@@ -500,11 +520,11 @@
             in_specs=[vmem] * 4,
             out_specs=vmem,
             scratch_shapes=[
-                pltpu.VMEM((2, groups_got // 4, 128), F32),
-                pltpu.VMEM((3, groups_got // 4, 128), jnp.int32),
-                pltpu.VMEM((2 * G // nc, G), F32),
-                pltpu.VMEM((2, 2 * G // nc, 512), BF16),
-                pltpu.VMEM((2, G, 512), BF16),
+                pltpu.VMEM((2, groups_left // 4, 128), F32),
+                pltpu.VMEM((3, groups_left // 4, 128), jnp.int32),
+                pltpu.VMEM((G, 2 * G // nc), F32),
+                pltpu.VMEM((2 * G // nc, 512), BF16),
+                pltpu.VMEM((G, 512), BF16),
             ],
             compiler_params=pltpu.CompilerParams(vmem_limit_bytes=40 << 20),
         )(got, edge, table, begun)

time: 25.2 us -> 23.4 us (0.929)
  Pallas kernels: 23.8 us -> 21.9 us
    pallas_call x1, Pallas kernels: 4.06 us -> 2.45 us  [usual(): pl.pallas_call(owned_rows, out_shape=jax.ShapeDtypeStruct((G // nc, 2, G)...]
where the time goes in v5:
time: 23.4 us; the launch traced here: 23.2 us
  Pallas kernels  21.9 us (94%)
  between operations  1.22 us (5%)
    pallas_call x1, Pallas kernels, per_device(): pl.pallas_call(exchange, out_shape=(jax.ShapeDtypeStruct((nc, 4 * GROUPS_...  19.5 us
    pallas_call x1, Pallas kernels, usual(): pl.pallas_call(owned_rows, out_shape=jax.ShapeDtypeStruct((G // nc, 2, G)...  2.45 us

profile of v5, /device:TPU:8, one launch (start us, length us, event | category | flops | bytes accessed | tf_op | source)
XLA Modules:
  0.0 23.2 jit_solution(13926434032075885915)
XLA Ops:
  0.7 19.5 %shard_map.57 = (f32[16,16,256]{2,1,0:T(8,128)S(1)}, f32[16,8,256]{2,1,0:T(8,128)S(1)}, bf16[64,64]{1,0:T(8,128)(2,1)S(1)}, f32[1024,128]{1,0:T(8,128)S(1)}, s32[1,1]{1,0:T(1,128)}) custom-call(f32[1,1,2,2048]{3,2,1,0:T(2,128)} %vis.1, s32[1,1,2,2048]{3,2,1,0:T(2,128)} %cell.1, s32[1,1,2048]{2,1,0:T(1,128)} %sup.1, s32[1,1,2048]{2,1,0:T(1,128)} %wpl.1, ...), custom_call_target="tpu_custom_call" | custom-call | tf_op jit(solution)/shard_map/pallas_call | solution.py:480
  20.7 2.5 %conditional.1 = (f32[64,2,1024]{2,1,0:T(2,128)}) conditional(s32[]{:T(128)} %bitcast.9, (f32[16,16,256]{2,1,0:T(8,128)S(1)}, f32[16,8,256]{2,1,0:T(8,128)S(1)}, bf16[64,64]{1,0:T(8,128)(2,1)S(1)}, f32[1024,128]{1,0:T(8,128)S(1)}) %tuple.27, (s32[1,1]{1,0:T(1,128)}, f32[1,1,2,2048]{3,2,1,0:T(2,128)}, s32[1,1,2,2048]{3,2,1,0:T(2,128)}, ...), branch_computations={%region_0.0_spmd, %region_1.6_spmd} | conditional | flops 334978816 | bytes 18040382 | solution.py:532
  20.7 2.4 %branch_0_fun.1 = f32[64,2,1024]{2,1,0:T(2,128)} custom-call(f32[16,16,256]{2,1,0:T(8,128)S(1)} %get-tuple-element.106.got, f32[16,8,256]{2,1,0:T(8,128)S(1)} %get-tuple-element.107.edge, bf16[64,64]{1,0:T(8,128)(2,1)S(1)} %get-tuple-element.108.table, f32[1024,128]{1,0:T(8,128)S(1)} %get-tuple-element.109.begun), custom_call_target="tpu_custom_call" | custom-call | tf_op jit(solution)/shard_map/cond/branch_0_fun/pallas_call | solution.py:517

commit v6 on v5

--- a/solution.py
+++ b/solution.py
@@ -163,7 +163,7 @@
         columns[...], weights[...], (((1,), (1,)), ((), ())), preferred_element_type=F32)
 
 
-def exchange(vis, cell, sup, wpl, cnt, got, edge, table, total, flag, vis_v, cell_v, sup_v, wpl_v, packed, tile_flags, chan_flags,
+def exchange(vis, cell, sup, wpl, cnt, got, edge, table, total, flag, vis_v, cell_v, sup_v, wpl_v, cnt_v, packed, tile_flags, chan_flags,
              weights, columns,
              load_sem, send_sem, recv_sem, edge_send, edge_recv, tf_send, tf_recv, cf_send, cf_recv):
     t, c = lax.axis_index("tile"), lax.axis_index("chan")
@@ -174,6 +174,7 @@
         pltpu.make_async_copy(cell.at[0, 0], cell_v, load_sem.at[1]),
         pltpu.make_async_copy(sup.at[0], sup_v, load_sem.at[2]),
         pltpu.make_async_copy(wpl.at[0], wpl_v, load_sem.at[3]),
+        pltpu.make_async_copy(cnt, cnt_v, load_sem.at[4]),
     ]
     for load in loads:
         load.start()
@@ -200,7 +201,7 @@
     for load in loads:
         load.wait()
 
-    live = lax.broadcasted_iota(jnp.int32, (1, slots), 1) < cnt[0, 0]
+    live = lax.broadcasted_iota(jnp.int32, (1, slots), 1) < cnt_v[...]
     row = cell_v[0:1]
     buckets = G // BUCKET
     bucket = row // BUCKET
@@ -248,25 +249,35 @@
 
     re_hi, re_lo = halves(vis_v[0:1])
     im_hi, im_lo = halves(vis_v[1:2])
-    col_hi, col_lo = halves(cell_v[1:2].astype(F32))
-    pieces = [re_hi, im_hi, col_hi, (row % BUCKET).astype(F32), sup_v[...].astype(F32), wpl_v[...].astype(F32),
-              jnp.ones((1, slots), F32), jnp.zeros((1, slots), F32), re_lo, im_lo, col_lo, jnp.zeros((1, slots), F32)]
-    spread = jnp.concatenate([jnp.where(at_place, x, 0.0).astype(BF16) for x in pieces], axis=0)
+    col = cell_v[1:2]
+    pieces = [re_hi, im_hi, col >> 2, sup_v[...] * PLANES + wpl_v[...], re_lo, im_lo,
+              (col & 3) * 64 + (row & (BUCKET - 1)) + 1, jnp.zeros((1, slots), F32)]
+    spread = jnp.concatenate([jnp.where(at_place, x.astype(F32), 0.0).astype(BF16) for x in pieces], axis=0)
     moved = lax.dot_general(to_group, spread, (((1,), (1,)), ((), ())), preferred_element_type=F32)
-    packed[:, 0:128] = moved[:, 0:128] + moved[:, 256:384]
-    packed[:, 128:256] = moved[:, 128:256]
+    first, second = moved[:, 0:128], moved[:, 128:256]
+    whole_1, whole_2 = first.astype(jnp.int32), second.astype(jnp.int32)
+    lane = lax.broadcasted_iota(jnp.int32, first.shape, 1) // LOW
+    packed[:, 0:128] = jnp.where(
+        lane < 2, first + second,
+        jnp.where(lane == 2, whole_1 * 4 + (whole_2 >> 6), pltpu.roll(whole_2, LOW, 1) & 63).astype(F32))
+    klass = pltpu.roll(whole_1, LOW, 1)
+    packed[:, 128:256] = jnp.where(
+        lane == 0, klass >> 4,
+        jnp.where(lane == 1, pltpu.roll(klass, LOW, 1) & (PLANES - 1),
+                  jnp.where((lane == 2) & ((whole_2 & 63) > 0), 1, 0))).astype(F32)
 
     width = 4 * GROUPS_IN
 
-    def payload(i, slot):
-        peer = lax.rem(c + i, nc)
+    def payload(peer, slot):
         return pltpu.make_async_remote_copy(
-            src_ref=packed.at[pl.ds(pl.multiple_of(8 * peer, 8), width)], dst_ref=got.at[slot], send_sem=send_sem.at[i],
+            src_ref=packed.at[pl.ds(8 * peer, width)], dst_ref=got.at[slot], send_sem=send_sem.at[peer],
             recv_sem=recv_sem.at[slot], device_id=(t, peer), device_id_type=MESH)
 
-    order = [8, 7, 9, 6, 10, 5, 11, 4, 12, 3, 13, 2, 14, 1, 15]
-    for i in order:
-        payload(i, c).start()
+    order = [0, 1, 2, 3, 4, 5, 8, 9, 6, 7, 10, 11, 12, 13, 14, 15]
+    for peer in order:
+        @pl.when(c != peer)
+        def _(peer=peer):
+            payload(peer, c).start()
 
     def edge_up():
         return pltpu.make_async_remote_copy(
@@ -292,13 +303,15 @@
         tile_flag(i, lax.rem(t + i, nt)).wait_recv()
     chan_flags[c] = jnp.max(tile_flags[...], axis=0)
 
-    def chan_flag(i, slot):
+    def chan_flag(peer, slot):
         return pltpu.make_async_remote_copy(
-            src_ref=chan_flags.at[c], dst_ref=chan_flags.at[slot], send_sem=cf_send.at[i], recv_sem=cf_recv.at[slot],
-            device_id=(t, lax.rem(c + i, nc)), device_id_type=MESH)
-
-    for i in order:
-        chan_flag(i, c).start()
+            src_ref=chan_flags.at[c], dst_ref=chan_flags.at[slot], send_sem=cf_send.at[peer], recv_sem=cf_recv.at[slot],
+            device_id=(t, peer), device_id_type=MESH)
+
+    for peer in order:
+        @pl.when(c != peer)
+        def _(peer=peer):
+            chan_flag(peer, c).start()
 
     table[...] = class_table()
     total[...] = jnp.zeros_like(total)
@@ -325,7 +338,7 @@
         return lines(klass, 0), lines(cells, 3), lines(cells, 2), lines(first, 0), lines(first, 1)
 
     halves_at = (0, G // 64 - SPAN)
-    lift = BUCKET * (lax.broadcasted_iota(jnp.int32, (width, 128), 0) // GROUPS_IN - 1)
+    lift = BUCKET * (lax.broadcasted_iota(jnp.int32, (width, 128), 0) // GROUPS_IN - 1) - 1
 
     here = 2 * (c // 2)
 
@@ -383,7 +396,7 @@
         rows = edge[...].reshape(nc * 8, 256)
         lines = nc // 4
         picks = [[8 * (4 * n + b) + g for b in range(4)] for g in EARLY for n in range(lines)]
-        made = fields(rows[:, 0:128], rows[:, 128:256], jnp.where(from_low, -BUCKET, 2 * BUCKET), picks)
+        made = fields(rows[:, 0:128], rows[:, 128:256], jnp.where(from_low, -BUCKET, 2 * BUCKET) - 1, picks)
         for h in range(2):
             for n in range(0, lines, 2):
                 lay(*[jnp.concatenate(x[h * lines + n : h * lines + n + 2], axis=1) for x in made], table,
@@ -391,14 +404,16 @@
         for n in range(lines // 2):
             add_both(n)
 
-    for i in range(1, nc):
-        chan_flag(i, lax.rem(c + i, nc)).wait_recv()
+    for peer in range(nc):
+        @pl.when(c != peer)
+        def _(peer=peer):
+            chan_flag(peer, peer).wait_recv()
+            chan_flag(peer, c).wait_send()
+            payload(peer, c).wait_send()
+
     flag[0, 0] = (jnp.max(jnp.max(chan_flags[...], axis=0)) > 0.5).astype(jnp.int32)
     for i in range(1, nt):
         tile_flag(i, t).wait_send()
-    for i in range(1, nc):
-        payload(i, c).wait_send()
-        chan_flag(i, c).wait_send()
 
     @pl.when(t < nt - 1)
     def _():
@@ -421,7 +436,7 @@
     both = jnp.concatenate([got[...].reshape(main, 256), edge[...].reshape(nc * 8, 256)], axis=0)
     index = lax.broadcasted_iota(jnp.int32, (count, 256), 0)
     shift = jnp.where(index < main, BUCKET * ((index % per) // GROUPS_IN - 1), jnp.where(c == 0, -BUCKET, 2 * BUCKET))
-    both = both + jnp.where(lanes == 3, shift, 0).astype(F32)
+    both = both + jnp.where(lanes == 3, shift - 1, 0).astype(F32)
     used = jnp.max(both[:, 128:256].T[2 * LOW : 3 * LOW], axis=0, keepdims=True)
     at = lax.broadcasted_iota(jnp.int32, (1, count), 1) % GROUPS_IN
     used = jnp.where((at == EARLY[0]) | (at == EARLY[1]), 0.0, used)
@@ -486,19 +501,20 @@
             jax.ShapeDtypeStruct((G, 2 * G // nc), F32),
             jax.ShapeDtypeStruct((1, 1), jnp.int32),
         ),
-        in_specs=[pl.BlockSpec(memory_space=pl.ANY)] * 4 + [pl.BlockSpec(memory_space=pltpu.SMEM)],
+        in_specs=[pl.BlockSpec(memory_space=pltpu.MemorySpace.HBM)] * 5,
         out_specs=(vmem, vmem, vmem, vmem, pl.BlockSpec(memory_space=pltpu.SMEM)),
         scratch_shapes=[
             pltpu.VMEM((2, slots), F32),
             pltpu.VMEM((2, slots), jnp.int32),
             pltpu.VMEM((1, slots), jnp.int32),
             pltpu.VMEM((1, slots), jnp.int32),
+            pltpu.VMEM((1, 1), jnp.int32),
             pltpu.VMEM((groups, FIELDS * LOW), F32),
             pltpu.VMEM((nt, 1, 128), F32),
             pltpu.VMEM((nc, 1, 128), F32),
             pltpu.VMEM((2, 2, 2 * G // nc, 256), BF16),
             pltpu.VMEM((2, 2, 64 * SPAN, 256), BF16),
-            pltpu.SemaphoreType.DMA((4,)),
+            pltpu.SemaphoreType.DMA((5,)),
             pltpu.SemaphoreType.DMA((nc,)),
             pltpu.SemaphoreType.DMA((nc,)),
             pltpu.SemaphoreType.DMA((2,)),

time: 23.4 us -> 23.4 us (level)
  no operation moved by 1% of the time
where the time goes in v6:
time: 23.4 us; the launch traced here: 23.1 us
  Pallas kernels  21.9 us (94%)
  between operations  1.22 us (5%)
    pallas_call x1, Pallas kernels, per_device(): pl.pallas_call(exchange, out_shape=(jax.ShapeDtypeStruct((nc, 4 * GROUPS_...  19.5 us
    pallas_call x1, Pallas kernels, usual(): pl.pallas_call(owned_rows, out_shape=jax.ShapeDtypeStruct((G // nc, 2, G)...  2.45 us

profile of v6, /device:TPU:8, one launch (start us, length us, event | category | flops | bytes accessed | tf_op | source)
XLA Modules:
  0.0 23.1 jit_solution(16841374572288910121)
XLA Ops:
  0.7 19.5 %shard_map.57 = (f32[16,16,256]{2,1,0:T(8,128)S(1)}, f32[16,8,256]{2,1,0:T(8,128)S(1)}, bf16[64,64]{1,0:T(8,128)(2,1)S(1)}, f32[1024,128]{1,0:T(8,128)S(1)}, s32[1,1]{1,0:T(1,128)}) custom-call(f32[1,1,2,2048]{3,2,1,0:T(2,128)} %vis.1, s32[1,1,2,2048]{3,2,1,0:T(2,128)} %cell.1, s32[1,1,2048]{2,1,0:T(1,128)} %sup.1, s32[1,1,2048]{2,1,0:T(1,128)} %wpl.1, ...), custom_call_target="tpu_custom_call" | custom-call | tf_op jit(solution)/shard_map/pallas_call | solution.py:495
  20.7 2.5 %conditional.1 = (f32[64,2,1024]{2,1,0:T(2,128)}) conditional(s32[]{:T(128)} %bitcast.9, (f32[16,16,256]{2,1,0:T(8,128)S(1)}, f32[16,8,256]{2,1,0:T(8,128)S(1)}, bf16[64,64]{1,0:T(8,128)(2,1)S(1)}, f32[1024,128]{1,0:T(8,128)S(1)}) %tuple.27, (s32[1,1]{1,0:T(1,128)}, f32[1,1,2,2048]{3,2,1,0:T(2,128)}, s32[1,1,2,2048]{3,2,1,0:T(2,128)}, ...), branch_computations={%region_0.0_spmd, %region_1.6_spmd} | conditional | flops 334978816 | bytes 18040382 | solution.py:548
  20.7 2.5 %branch_0_fun.1 = f32[64,2,1024]{2,1,0:T(2,128)} custom-call(f32[16,16,256]{2,1,0:T(8,128)S(1)} %get-tuple-element.106.got, f32[16,8,256]{2,1,0:T(8,128)S(1)} %get-tuple-element.107.edge, bf16[64,64]{1,0:T(8,128)(2,1)S(1)} %get-tuple-element.108.table, f32[1024,128]{1,0:T(8,128)S(1)} %get-tuple-element.109.begun), custom_call_target="tpu_custom_call" | custom-call | tf_op jit(solution)/shard_map/cond/branch_0_fun/pallas_call | solution.py:533

commit v7 on v6

--- a/solution.py
+++ b/solution.py
@@ -18,7 +18,7 @@
 LOW = 32
 GROUPS_IN = CAP // LOW
 EARLY = (0, GROUPS_IN - 1)
-SPAN = 9
+SPAN = 10
 FIELDS = 8
 MESH = pl.DeviceIdType.MESH
 F32 = jnp.float32
@@ -159,11 +159,56 @@
 
 def add(total, weights, columns, start=0):
     stop = 64 * start + columns.shape[0]
-    total[64 * start : stop] += lax.dot_general(
-        columns[...], weights[...], (((1,), (1,)), ((), ())), preferred_element_type=F32)
-
-
-def exchange(vis, cell, sup, wpl, cnt, got, edge, table, total, flag, vis_v, cell_v, sup_v, wpl_v, cnt_v, packed, tile_flags, chan_flags,
+    total[:, 64 * start : stop] += lax.dot_general(
+        weights[...], columns[...], (((1,), (1,)), ((), ())), preferred_element_type=F32)
+
+
+def list_left(got, edge, real, whole, number):
+    c = lax.axis_index("chan")
+    nc, per = got.shape[0], got.shape[1]
+    main = nc * per
+    count = main + nc * 8
+    left = 4 * real.shape[1]
+    quarter = left // 4
+
+    lanes = lax.broadcasted_iota(jnp.int32, (1, 256), 1) // LOW
+    both = jnp.concatenate([got[...].reshape(main, 256), edge[...].reshape(nc * 8, 256)], axis=0)
+    index = lax.broadcasted_iota(jnp.int32, (count, 256), 0)
+    shift = jnp.where(index < main, BUCKET * ((index % per) // GROUPS_IN - 1), jnp.where(c == 0, -BUCKET, 2 * BUCKET))
+    both = both + jnp.where(lanes == 3, shift - 1, 0).astype(F32)
+    used = jnp.max(both[:, 128:256].T[2 * LOW : 3 * LOW], axis=0, keepdims=True)
+    at = lax.broadcasted_iota(jnp.int32, (1, count), 1) % GROUPS_IN
+    used = jnp.where((at == EARLY[0]) | (at == EARLY[1]), 0.0, used)
+    before = (
+        lax.broadcasted_iota(jnp.int32, (count, count), 0) < lax.broadcasted_iota(jnp.int32, (count, count), 1)
+    ).astype(F32).astype(BF16)
+    rank = jnp.dot(jnp.broadcast_to(used, (8, count)).astype(BF16), before, preferred_element_type=F32)[0:1]
+    rank = jnp.where(used > 0.5, rank, -1.0)
+    place = lax.broadcasted_iota(jnp.int32, (left, count), 0)
+    place = (4 * (place % quarter) + place // quarter).astype(F32)
+    pick = jnp.where(place == rank, 1.0, 0.0).astype(BF16)
+    high = both.astype(BF16)
+    low = (both - high.astype(F32)).astype(BF16)
+    rows = jnp.dot(pick, high, preferred_element_type=F32) + jnp.dot(pick, low, preferred_element_type=F32)
+    spot = lax.broadcasted_iota(jnp.int32, (quarter, 128), 1) // LOW
+
+    def field(f):
+        part, offset = divmod(f, 4)
+        result = None
+        for s in range(4):
+            x = rows[s * quarter : (s + 1) * quarter, 128 * part : 128 * part + 128]
+            if (s - offset) % 4:
+                x = pltpu.roll(x, ((s - offset) % 4) * LOW, 1)
+            result = x if result is None else jnp.where(spot == s, x, result)
+        return result
+
+    real[0], real[1] = field(0), field(1)
+    whole[0], whole[1] = field(2).astype(jnp.int32) - M, field(3).astype(jnp.int32) - M
+    whole[2] = (field(4) * float(PLANES) + field(5)).astype(jnp.int32)
+    number[...] = jnp.broadcast_to(jnp.sum(used, axis=1, keepdims=True), number.shape)
+
+
+def exchange(vis, cell, sup, wpl, cnt, table, total, real, whole, number, flag, got, edge, vis_v, cell_v, sup_v, wpl_v, cnt_v, packed, tile_flags, chan_flags,
              weights, columns,
              load_sem, send_sem, recv_sem, edge_send, edge_recv, tf_send, tf_recv, cf_send, cf_recv):
     t, c = lax.axis_index("tile"), lax.axis_index("chan")
@@ -380,12 +425,7 @@
 
     chips = nc // 2
     lax.fori_loop(0, chips // 2 - 1, two_chips, 0)
-    source = chip(chips - 1)
-    arrive(source)
-    arrive(source + 1)
-    prepare(source, 1)
     add_both(0)
-    add_both(1)
 
     @pl.when(from_low | from_high)
     def _():
@@ -404,6 +444,13 @@
         for n in range(lines // 2):
             add_both(n)
 
+    source = chip(chips - 1)
+    arrive(source)
+    arrive(source + 1)
+    prepare(source, 1)
+    list_left(got, edge, real, whole, number)
+    add_both(1)
+
     for peer in range(nc):
         @pl.when(c != peer)
         def _(peer=peer):
@@ -424,52 +471,10 @@
         edge_down().wait_send()
 
 
-def owned_rows(got, edge, table, begun, out, real, whole, total, weights, columns):
-    c = lax.axis_index("chan")
-    nc, per = got.shape[0], got.shape[1]
-    main = nc * per
-    count = main + nc * 8
-    left = nc * (per // GROUPS_IN + 1) * (GROUPS_IN - len(EARLY))
-    quarter = left // 4
-
-    lanes = lax.broadcasted_iota(jnp.int32, (1, 256), 1) // LOW
-    both = jnp.concatenate([got[...].reshape(main, 256), edge[...].reshape(nc * 8, 256)], axis=0)
-    index = lax.broadcasted_iota(jnp.int32, (count, 256), 0)
-    shift = jnp.where(index < main, BUCKET * ((index % per) // GROUPS_IN - 1), jnp.where(c == 0, -BUCKET, 2 * BUCKET))
-    both = both + jnp.where(lanes == 3, shift - 1, 0).astype(F32)
-    used = jnp.max(both[:, 128:256].T[2 * LOW : 3 * LOW], axis=0, keepdims=True)
-    at = lax.broadcasted_iota(jnp.int32, (1, count), 1) % GROUPS_IN
-    used = jnp.where((at == EARLY[0]) | (at == EARLY[1]), 0.0, used)
-    before = (
-        lax.broadcasted_iota(jnp.int32, (count, count), 0) < lax.broadcasted_iota(jnp.int32, (count, count), 1)
-    ).astype(F32).astype(BF16)
-    rank = jnp.dot(jnp.broadcast_to(used, (8, count)).astype(BF16), before, preferred_element_type=F32)[0:1]
-    rank = jnp.where(used > 0.5, rank, -1.0)
-    place = lax.broadcasted_iota(jnp.int32, (left, count), 0)
-    place = (4 * (place % quarter) + place // quarter).astype(F32)
-    pick = jnp.where(place == rank, 1.0, 0.0).astype(BF16)
-    high = both.astype(BF16)
-    low = (both - high.astype(F32)).astype(BF16)
-    rows = jnp.dot(pick, high, preferred_element_type=F32) + jnp.dot(pick, low, preferred_element_type=F32)
-    spot = lax.broadcasted_iota(jnp.int32, (quarter, 128), 1) // LOW
-
-    def field(f):
-        part, offset = divmod(f, 4)
-        result = None
-        for s in range(4):
-            x = rows[s * quarter : (s + 1) * quarter, 128 * part : 128 * part + 128]
-            if (s - offset) % 4:
-                x = pltpu.roll(x, ((s - offset) % 4) * LOW, 1)
-            result = x if result is None else jnp.where(spot == s, x, result)
-        return result
-
-    real[0], real[1] = field(0), field(1)
-    whole[0], whole[1] = field(2).astype(jnp.int32) - M, field(3).astype(jnp.int32) - M
-    whole[2] = (field(4) * float(PLANES) + field(5)).astype(jnp.int32)
+def owned_rows(real, whole, number, table, begun, out, total, weights, columns):
     size = weights.shape[-1]
     lines = size // 128
-    chunks = (jnp.sum(used).astype(jnp.int32) + 4 * lines - 1) // (4 * lines)
-
+    chunks = (jnp.max(number[...]).astype(jnp.int32) + 4 * lines - 1) // (4 * lines)
     total[...] = begun[...]
 
     def body(i, carry):
@@ -482,9 +487,8 @@
         return carry
 
     lax.fori_loop(0, chunks, body, 0)
-    rows = total[...].T
-    out[:, 0, :] = rows[0:64]
-    out[:, 1, :] = rows[64:128]
+    out[:, 0, :] = total[0:64]
+    out[:, 1, :] = total[64:128]
 
 
 def per_device(visibilities, cell_offsets, support_index, w_plane, live_counts):
@@ -492,18 +496,22 @@
     slots = visibilities.shape[-1]
     groups = (G // BUCKET + 2) * GROUPS_IN
     vmem = pl.BlockSpec(memory_space=pltpu.VMEM)
-    got, edge, table, begun, flag = pl.pallas_call(
+    left_lines = nc * 5 * (GROUPS_IN - len(EARLY)) // 4
+    table, begun, real, whole, number, flag = pl.pallas_call(
         exchange,
         out_shape=(
-            jax.ShapeDtypeStruct((nc, 4 * GROUPS_IN, FIELDS * LOW), F32),
-            jax.ShapeDtypeStruct((nc, 8, FIELDS * LOW), F32),
             jax.ShapeDtypeStruct((2 * M, 4 * PLANES), BF16),
-            jax.ShapeDtypeStruct((G, 2 * G // nc), F32),
+            jax.ShapeDtypeStruct((2 * G // nc, G), F32),
+            jax.ShapeDtypeStruct((2, left_lines, 128), F32),
+            jax.ShapeDtypeStruct((3, left_lines, 128), jnp.int32),
+            jax.ShapeDtypeStruct((8, 128), F32),
             jax.ShapeDtypeStruct((1, 1), jnp.int32),
         ),
         in_specs=[pl.BlockSpec(memory_space=pltpu.MemorySpace.HBM)] * 5,
-        out_specs=(vmem, vmem, vmem, vmem, pl.BlockSpec(memory_space=pltpu.SMEM)),
+        out_specs=(vmem, vmem, vmem, vmem, vmem, pl.BlockSpec(memory_space=pltpu.SMEM)),
         scratch_shapes=[
+            pltpu.VMEM((nc, 4 * GROUPS_IN, FIELDS * LOW), F32),
+            pltpu.VMEM((nc, 8, FIELDS * LOW), F32),
             pltpu.VMEM((2, slots), F32),
             pltpu.VMEM((2, slots), jnp.int32),
             pltpu.VMEM((1, slots), jnp.int32),
@@ -527,23 +535,20 @@
         compiler_params=pltpu.CompilerParams(collective_id=0, has_side_effects=True, vmem_limit_bytes=62 << 20),
     )(visibilities, cell_offsets, support_index, w_plane, live_counts)
 
-    groups_left = nc * 5 * (GROUPS_IN - len(EARLY))
 
     def usual(*_):
         return pl.pallas_call(
             owned_rows,
             out_shape=jax.ShapeDtypeStruct((G // nc, 2, G), F32),
-            in_specs=[vmem] * 4,
+            in_specs=[vmem] * 5,
             out_specs=vmem,
             scratch_shapes=[
-                pltpu.VMEM((2, groups_left // 4, 128), F32),
-                pltpu.VMEM((3, groups_left // 4, 128), jnp.int32),
-                pltpu.VMEM((G, 2 * G // nc), F32),
+                pltpu.VMEM((2 * G // nc, G), F32),
                 pltpu.VMEM((2 * G // nc, 512), BF16),
                 pltpu.VMEM((G, 512), BF16),
             ],
             compiler_params=pltpu.CompilerParams(vmem_limit_bytes=40 << 20),
-        )(got, edge, table, begun)
+        )(real, whole, number, table, begun)
 
     return lax.cond(
         flag[0, 0] > 0, any_cells, usual, visibilities, cell_offsets, support_index, w_plane, live_counts

time: 23.4 us -> 23.3 us (level)
    pallas_call x1, Pallas kernels: 2.45 us -> 1.72 us  [usual(): pl.pallas_call(owned_rows, out_shape=jax.ShapeDtypeStruct((G // nc, 2, G)...]
    pallas_call x1, Pallas kernels: 19.5 us -> 20.1 us  [per_device(): pl.pallas_call(exchange, out_shape=(jax.ShapeDtypeStruct((2 * M, 4 * PLAN...]
where the time goes in v7:
time: 23.3 us; the launch traced here: 23 us
  Pallas kernels  21.8 us (94%)
  between operations  1.22 us (5%)
    pallas_call x1, Pallas kernels, per_device(): pl.pallas_call(exchange, out_shape=(jax.ShapeDtypeStruct((2 * M, 4 * PLAN...  20.1 us
    pallas_call x1, Pallas kernels, usual(): pl.pallas_call(owned_rows, out_shape=jax.ShapeDtypeStruct((G // nc, 2, G)...  1.72 us

profile of v7, /device:TPU:8, one launch (start us, length us, event | category | flops | bytes accessed | tf_op | source)
XLA Modules:
  0.0 23.0 jit_solution(3947920483784968010)
XLA Ops:
  0.7 20.1 %shard_map.57 = (bf16[64,64]{1,0:T(8,128)(2,1)S(1)}, f32[128,1024]{1,0:T(8,128)S(1)}, f32[2,40,128]{2,1,0:T(8,128)S(1)}, s32[3,40,128]{2,1,0:T(8,128)S(1)}, f32[8,128]{1,0:T(8,128)S(1)}, /*index=5*/s32[1,1]{1,0:T(1,128)}) custom-call(f32[1,1,2,2048]{3,2,1,0:T(2,128)} %vis.1, s32[1,1,2,2048]{3,2,1,0:T(2,128)} %cell.1, s32[1,1,2048]{2,1,0:T(1,128)} %sup.1, ...), custom_call_target="tpu_custom_call" | custom-call | tf_op jit(solution)/shard_map/pallas_call | solution.py:500
  21.3 1.7 %conditional.1 = (f32[64,2,1024]{2,1,0:T(2,128)}) conditional(s32[]{:T(128)} %bitcast.9, (f32[2,40,128]{2,1,0:T(8,128)S(1)}, s32[3,40,128]{2,1,0:T(8,128)S(1)}, f32[8,128]{1,0:T(8,128)S(1)}, bf16[64,64]{1,0:T(8,128)(2,1)S(1)}, f32[128,1024]{1,0:T(8,128)S(1)}) %tuple.27, (s32[1,1]{1,0:T(1,128)}, f32[1,1,2,2048]{3,2,1,0:T(2,128)}, ...), branch_computations={%region_0.0_spmd, %region_1.6_spmd} | conditional | flops 334978816 | bytes 18040382 | solution.py:553
  21.3 1.7 %branch_0_fun.1 = f32[64,2,1024]{2,1,0:T(2,128)} custom-call(f32[2,40,128]{2,1,0:T(8,128)S(1)} %get-tuple-element.108.real, s32[3,40,128]{2,1,0:T(8,128)S(1)} %get-tuple-element.109.whole, f32[8,128]{1,0:T(8,128)S(1)} %get-tuple-element.110.number, bf16[64,64]{1,0:T(8,128)(2,1)S(1)} %get-tuple-element.111.table, f32[128,1024]{1,0:T(8,128)S(1)} %get-tuple-element.112.begun), custom_call_target="tpu_custom_call" | custom-call | tf_op jit(solution)/shard_map/cond/branch_0_fun/pallas_call | solution.py:540

commit v8 on v7

--- a/solution.py
+++ b/solution.py
@@ -128,13 +128,10 @@
     for bit in (32, 16, 8):
         chosen = (by & bit) != 0
         values = [jnp.where(chosen, values[(k - bit // 8) % 8], values[k]) for k in range(8)]
-    for bit in (4, 2, 1):
-        chosen = (by & bit) != 0
-        rolled = [pltpu.roll(x, bit, 0) for x in values]
-        values = [
-            jnp.where(chosen, jnp.where(sub < bit, rolled[(k - 1) % 8], rolled[k]), values[k]) for k in range(8)
-        ]
-    return values
+    fine = by & 7
+    taken = [jnp.take_along_axis(x, (sub - fine) & 7, axis=0, mode="promise_in_bounds") for x in values]
+    wrapped = sub < fine
+    return [jnp.where(wrapped, taken[(k - 1) % 8], taken[k]) for k in range(8)]
 
 
 def lay(klass, row, col, re, im, table, weights, columns, start=0):
@@ -550,8 +547,8 @@
             compiler_params=pltpu.CompilerParams(vmem_limit_bytes=40 << 20),
         )(real, whole, number, table, begun)
 
-    return lax.cond(
-        flag[0, 0] > 0, any_cells, usual, visibilities, cell_offsets, support_index, w_plane, live_counts
+    return lax.switch(
+        flag[0, 0], (usual, any_cells), visibilities, cell_offsets, support_index, w_plane, live_counts
     )
 
 

time: 23.3 us -> 22.4 us (0.961)
  Pallas kernels: 21.8 us -> 21 us
    pallas_call x1, Pallas kernels: 20.1 us -> 19.3 us  [per_device(): pl.pallas_call(exchange, out_shape=(jax.ShapeDtypeStruct((2 * M, 4 * PLAN...]
where the time goes in v8:
time: 22.4 us; the launch traced here: 22.2 us
  Pallas kernels  21 us (94%)
  between operations  1.22 us (5%)
    pallas_call x1, Pallas kernels, per_device(): pl.pallas_call(exchange, out_shape=(jax.ShapeDtypeStruct((2 * M, 4 * PLAN...  19.3 us
    pallas_call x1, Pallas kernels, usual(): pl.pallas_call(owned_rows, out_shape=jax.ShapeDtypeStruct((G // nc, 2, G)...  1.66 us

profile of v8, /device:TPU:8, one launch (start us, length us, event | category | flops | bytes accessed | tf_op | source)
XLA Modules:
  0.0 22.2 jit_solution(8441429755139270046)
XLA Ops:
  0.7 19.3 %shard_map.57 = (bf16[64,64]{1,0:T(8,128)(2,1)S(1)}, f32[128,1024]{1,0:T(8,128)S(1)}, f32[2,40,128]{2,1,0:T(8,128)S(1)}, s32[3,40,128]{2,1,0:T(8,128)S(1)}, f32[8,128]{1,0:T(8,128)S(1)}, /*index=5*/s32[1,1]{1,0:T(1,128)}) custom-call(f32[1,1,2,2048]{3,2,1,0:T(2,128)} %vis.1, s32[1,1,2,2048]{3,2,1,0:T(2,128)} %cell.1, s32[1,1,2048]{2,1,0:T(1,128)} %sup.1, ...), custom_call_target="tpu_custom_call" | custom-call | tf_op jit(solution)/shard_map/pallas_call | solution.py:497
  20.5 1.7 %conditional.1 = (f32[64,2,1024]{2,1,0:T(2,128)}) conditional(s32[]{:T(128)} %bitcast.9, (f32[2,40,128]{2,1,0:T(8,128)S(1)}, s32[3,40,128]{2,1,0:T(8,128)S(1)}, f32[8,128]{1,0:T(8,128)S(1)}, bf16[64,64]{1,0:T(8,128)(2,1)S(1)}, f32[128,1024]{1,0:T(8,128)S(1)}) %tuple.27, (s32[1,1]{1,0:T(1,128)}, f32[1,1,2,2048]{3,2,1,0:T(2,128)}, ...), branch_computations={%region_0.0_spmd, %region_1.6_spmd} | conditional | flops 334978816 | bytes 18040382 | solution.py:550
  20.5 1.7 %branch_0_fun.1 = f32[64,2,1024]{2,1,0:T(2,128)} custom-call(f32[2,40,128]{2,1,0:T(8,128)S(1)} %get-tuple-element.108.real, s32[3,40,128]{2,1,0:T(8,128)S(1)} %get-tuple-element.109.whole, f32[8,128]{1,0:T(8,128)S(1)} %get-tuple-element.110.number, bf16[64,64]{1,0:T(8,128)(2,1)S(1)} %get-tuple-element.111.table, f32[128,1024]{1,0:T(8,128)S(1)} %get-tuple-element.112.begun), custom_call_target="tpu_custom_call" | custom-call | tf_op jit(solution)/shard_map/cond/branch_0_fun/pallas_call | solution.py:537

commit v9 on v8

--- a/solution.py
+++ b/solution.py
@@ -272,7 +272,7 @@
 
     def tile_flag(i, slot):
         return pltpu.make_async_remote_copy(
-            src_ref=tile_flags.at[t], dst_ref=tile_flags.at[slot], send_sem=tf_send.at[i], recv_sem=tf_recv.at[slot],
+            src_ref=tile_flags.at[t], dst_ref=tile_flags.at[slot], send_sem=tf_send, recv_sem=tf_recv,
             device_id=(lax.rem(t + i, nt), c), device_id_type=MESH)
 
     for i in range(1, nt):
@@ -312,7 +312,7 @@
 
     def payload(peer, slot):
         return pltpu.make_async_remote_copy(
-            src_ref=packed.at[pl.ds(8 * peer, width)], dst_ref=got.at[slot], send_sem=send_sem.at[peer],
+            src_ref=packed.at[pl.ds(8 * peer, width)], dst_ref=got.at[slot], send_sem=send_sem,
             recv_sem=recv_sem.at[slot], device_id=(t, peer), device_id_type=MESH)
 
     order = [0, 1, 2, 3, 4, 5, 8, 9, 6, 7, 10, 11, 12, 13, 14, 15]
@@ -341,13 +341,17 @@
 
     got[c] = packed[pl.ds(pl.multiple_of(8 * c, 8), width), :]
 
-    for i in range(1, nt):
-        tile_flag(i, lax.rem(t + i, nt)).wait_recv()
+    def all_of(ref, count, sent, landed):
+        return pltpu.make_async_remote_copy(
+            src_ref=ref.at[0:count], dst_ref=ref.at[0:count], send_sem=sent, recv_sem=landed,
+            device_id=(t, lax.rem(c + 1, nc)), device_id_type=MESH)
+
+    all_of(tile_flags, nt - 1, tf_send, tf_recv).wait_recv()
     chan_flags[c] = jnp.max(tile_flags[...], axis=0)
 
     def chan_flag(peer, slot):
         return pltpu.make_async_remote_copy(
-            src_ref=chan_flags.at[c], dst_ref=chan_flags.at[slot], send_sem=cf_send.at[peer], recv_sem=cf_recv.at[slot],
+            src_ref=chan_flags.at[c], dst_ref=chan_flags.at[slot], send_sem=cf_send, recv_sem=cf_recv,
             device_id=(t, peer), device_id_type=MESH)
 
     for peer in order:
@@ -405,7 +409,7 @@
 
     def arrive(source):
         pltpu.make_async_remote_copy(
-            src_ref=packed.at[pl.ds(0, width)], dst_ref=got.at[source], send_sem=send_sem.at[1],
+            src_ref=packed.at[pl.ds(0, width)], dst_ref=got.at[source], send_sem=send_sem,
             recv_sem=recv_sem.at[source], device_id=(t, source), device_id_type=MESH).wait_recv()
 
     arrive(here + (c + 1) % 2)
@@ -441,6 +445,18 @@
         for n in range(lines // 2):
             add_both(n)
 
+    all_of(tile_flags, nt - 1, tf_send, tf_recv).wait_send()
+    all_of(chan_flags, nc - 1, cf_send, cf_recv).wait_send()
+    all_of(got, nc - 1, send_sem, recv_sem.at[0]).wait_send()
+
+    @pl.when(t < nt - 1)
+    def _():
+        edge_up().wait_send()
+
+    @pl.when(t > 0)
+    def _():
+        edge_down().wait_send()
+
     source = chip(chips - 1)
     arrive(source)
     arrive(source + 1)
@@ -448,24 +464,8 @@
     list_left(got, edge, real, whole, number)
     add_both(1)
 
-    for peer in range(nc):
-        @pl.when(c != peer)
-        def _(peer=peer):
-            chan_flag(peer, peer).wait_recv()
-            chan_flag(peer, c).wait_send()
-            payload(peer, c).wait_send()
-
+    all_of(chan_flags, nc - 1, cf_send, cf_recv).wait_recv()
     flag[0, 0] = (jnp.max(jnp.max(chan_flags[...], axis=0)) > 0.5).astype(jnp.int32)
-    for i in range(1, nt):
-        tile_flag(i, t).wait_send()
-
-    @pl.when(t < nt - 1)
-    def _():
-        edge_up().wait_send()
-
-    @pl.when(t > 0)
-    def _():
-        edge_down().wait_send()
 
 
 def owned_rows(real, whole, number, table, begun, out, total, weights, columns):
@@ -520,14 +520,14 @@
             pltpu.VMEM((2, 2, 2 * G // nc, 256), BF16),
             pltpu.VMEM((2, 2, 64 * SPAN, 256), BF16),
             pltpu.SemaphoreType.DMA((5,)),
-            pltpu.SemaphoreType.DMA((nc,)),
+            pltpu.SemaphoreType.DMA,
             pltpu.SemaphoreType.DMA((nc,)),
             pltpu.SemaphoreType.DMA((2,)),
             pltpu.SemaphoreType.DMA((nc,)),
-            pltpu.SemaphoreType.DMA((nt,)),
-            pltpu.SemaphoreType.DMA((nt,)),
-            pltpu.SemaphoreType.DMA((nc,)),
-            pltpu.SemaphoreType.DMA((nc,)),
+            pltpu.SemaphoreType.DMA,
+            pltpu.SemaphoreType.DMA,
+            pltpu.SemaphoreType.DMA,
+            pltpu.SemaphoreType.DMA,
         ],
         compiler_params=pltpu.CompilerParams(collective_id=0, has_side_effects=True, vmem_limit_bytes=62 << 20),
     )(visibilities, cell_offsets, support_index, w_plane, live_counts)

time: 22.4 us -> 21.8 us (0.973)
  Pallas kernels: 21 us -> 20.3 us
    pallas_call x1, Pallas kernels: 19.3 us -> 18.7 us  [per_device(): pl.pallas_call(exchange, out_shape=(jax.ShapeDtypeStruct((2 * M, 4 * PLAN...]
where the time goes in v9:
time: 21.8 us; the launch traced here: 21.6 us
  Pallas kernels  20.3 us (93%)
  between operations  1.22 us (6%)
    pallas_call x1, Pallas kernels, per_device(): pl.pallas_call(exchange, out_shape=(jax.ShapeDtypeStruct((2 * M, 4 * PLAN...  18.7 us
    pallas_call x1, Pallas kernels, usual(): pl.pallas_call(owned_rows, out_shape=jax.ShapeDtypeStruct((G // nc, 2, G)...  1.67 us

profile of v9, /device:TPU:8, one launch (start us, length us, event | category | flops | bytes accessed | tf_op | source)
XLA Modules:
  0.0 21.6 jit_solution(3779588763260855114)
XLA Ops:
  0.7 18.7 %shard_map.57 = (bf16[64,64]{1,0:T(8,128)(2,1)S(1)}, f32[128,1024]{1,0:T(8,128)S(1)}, f32[2,40,128]{2,1,0:T(8,128)S(1)}, s32[3,40,128]{2,1,0:T(8,128)S(1)}, f32[8,128]{1,0:T(8,128)S(1)}, /*index=5*/s32[1,1]{1,0:T(1,128)}) custom-call(f32[1,1,2,2048]{3,2,1,0:T(2,128)} %vis.1, s32[1,1,2,2048]{3,2,1,0:T(2,128)} %cell.1, s32[1,1,2048]{2,1,0:T(1,128)} %sup.1, ...), custom_call_target="tpu_custom_call" | custom-call | tf_op jit(solution)/shard_map/pallas_call | solution.py:497
  19.9 1.7 %conditional.1 = (f32[64,2,1024]{2,1,0:T(2,128)}) conditional(s32[]{:T(128)} %bitcast.9, (f32[2,40,128]{2,1,0:T(8,128)S(1)}, s32[3,40,128]{2,1,0:T(8,128)S(1)}, f32[8,128]{1,0:T(8,128)S(1)}, bf16[64,64]{1,0:T(8,128)(2,1)S(1)}, f32[128,1024]{1,0:T(8,128)S(1)}) %tuple.27, (s32[1,1]{1,0:T(1,128)}, f32[1,1,2,2048]{3,2,1,0:T(2,128)}, ...), branch_computations={%region_0.0_spmd, %region_1.6_spmd} | conditional | flops 334978816 | bytes 18040382 | solution.py:550
  19.9 1.7 %branch_0_fun.1 = f32[64,2,1024]{2,1,0:T(2,128)} custom-call(f32[2,40,128]{2,1,0:T(8,128)S(1)} %get-tuple-element.108.real, s32[3,40,128]{2,1,0:T(8,128)S(1)} %get-tuple-element.109.whole, f32[8,128]{1,0:T(8,128)S(1)} %get-tuple-element.110.number, bf16[64,64]{1,0:T(8,128)(2,1)S(1)} %get-tuple-element.111.table, f32[128,1024]{1,0:T(8,128)S(1)} %get-tuple-element.112.begun), custom_call_target="tpu_custom_call" | custom-call | tf_op jit(solution)/shard_map/cond/branch_0_fun/pallas_call | solution.py:537

commit v10 on v9

--- a/solution.py
+++ b/solution.py
@@ -267,17 +267,6 @@
     over = full.astype(F32)
     tile_flags[t] = jnp.broadcast_to(over, (1, 128))
 
-    below, above = (t > 0).astype(jnp.int32), (t < nt - 1).astype(jnp.int32)
-    pl.semaphore_wait(bar, nc - 1 + nt - 1 + below + above)
-
-    def tile_flag(i, slot):
-        return pltpu.make_async_remote_copy(
-            src_ref=tile_flags.at[t], dst_ref=tile_flags.at[slot], send_sem=tf_send, recv_sem=tf_recv,
-            device_id=(lax.rem(t + i, nt), c), device_id_type=MESH)
-
-    for i in range(1, nt):
-        tile_flag(i, t).start()
-
     spot = jnp.where(right, CAP - 1 - rank, rank)
     group = jnp.where(live, (bucket + 1) * GROUPS_IN + (spot >> (LOW.bit_length() - 1)), -1)
     place = spot & (LOW - 1)
@@ -308,18 +297,27 @@
         jnp.where(lane == 1, pltpu.roll(klass, LOW, 1) & (PLANES - 1),
                   jnp.where((lane == 2) & ((whole_2 & 63) > 0), 1, 0))).astype(F32)
 
+    below, above = (t > 0).astype(jnp.int32), (t < nt - 1).astype(jnp.int32)
+    pl.semaphore_wait(bar, nc - 1 + nt - 1 + below + above)
+
+    def tile_flag(i, slot):
+        return pltpu.make_async_remote_copy(
+            src_ref=tile_flags.at[t], dst_ref=tile_flags.at[slot], send_sem=tf_send, recv_sem=tf_recv,
+            device_id=(lax.rem(t + i, nt), c), device_id_type=MESH)
+
+    for i in range(1, nt):
+        tile_flag(i, t).start()
+
     width = 4 * GROUPS_IN
 
-    def payload(peer, slot):
+    def payload(i, slot):
+        peer = lax.rem(c + i, nc)
         return pltpu.make_async_remote_copy(
-            src_ref=packed.at[pl.ds(8 * peer, width)], dst_ref=got.at[slot], send_sem=send_sem,
+            src_ref=packed.at[pl.ds(pl.multiple_of(8 * peer, 8), width)], dst_ref=got.at[slot], send_sem=send_sem,
             recv_sem=recv_sem.at[slot], device_id=(t, peer), device_id_type=MESH)
 
-    order = [0, 1, 2, 3, 4, 5, 8, 9, 6, 7, 10, 11, 12, 13, 14, 15]
-    for peer in order:
-        @pl.when(c != peer)
-        def _(peer=peer):
-            payload(peer, c).start()
+    for i in range(1, nc):
+        payload(i, c).start()
 
     def edge_up():
         return pltpu.make_async_remote_copy(
@@ -349,15 +347,10 @@
     all_of(tile_flags, nt - 1, tf_send, tf_recv).wait_recv()
     chan_flags[c] = jnp.max(tile_flags[...], axis=0)
 
-    def chan_flag(peer, slot):
-        return pltpu.make_async_remote_copy(
-            src_ref=chan_flags.at[c], dst_ref=chan_flags.at[slot], send_sem=cf_send, recv_sem=cf_recv,
-            device_id=(t, peer), device_id_type=MESH)
-
-    for peer in order:
-        @pl.when(c != peer)
-        def _(peer=peer):
-            chan_flag(peer, c).start()
+    for i in range(1, nc):
+        pltpu.make_async_remote_copy(
+            src_ref=chan_flags.at[c], dst_ref=chan_flags.at[c], send_sem=cf_send, recv_sem=cf_recv,
+            device_id=(t, lax.rem(c + i, nc)), device_id_type=MESH).start()
 
     table[...] = class_table()
     total[...] = jnp.zeros_like(total)

time: 21.8 us -> 21.8 us (level)
  no operation moved by 1% of the time
where the time goes in v10:
time: 21.8 us; the launch traced here: 21.6 us
  Pallas kernels  20.3 us (93%)
  between operations  1.22 us (6%)
    pallas_call x1, Pallas kernels, per_device(): pl.pallas_call(exchange, out_shape=(jax.ShapeDtypeStruct((2 * M, 4 * PLAN...  18.7 us
    pallas_call x1, Pallas kernels, usual(): pl.pallas_call(owned_rows, out_shape=jax.ShapeDtypeStruct((G // nc, 2, G)...  1.66 us

profile of v10, /device:TPU:8, one launch (start us, length us, event | category | flops | bytes accessed | tf_op | source)
XLA Modules:
  0.0 21.6 jit_solution(11930249295344886513)
XLA Ops:
  0.7 18.7 %shard_map.57 = (bf16[64,64]{1,0:T(8,128)(2,1)S(1)}, f32[128,1024]{1,0:T(8,128)S(1)}, f32[2,40,128]{2,1,0:T(8,128)S(1)}, s32[3,40,128]{2,1,0:T(8,128)S(1)}, f32[8,128]{1,0:T(8,128)S(1)}, /*index=5*/s32[1,1]{1,0:T(1,128)}) custom-call(f32[1,1,2,2048]{3,2,1,0:T(2,128)} %vis.1, s32[1,1,2,2048]{3,2,1,0:T(2,128)} %cell.1, s32[1,1,2048]{2,1,0:T(1,128)} %sup.1, ...), custom_call_target="tpu_custom_call" | custom-call | tf_op jit(solution)/shard_map/pallas_call | solution.py:490
  19.9 1.7 %conditional.1 = (f32[64,2,1024]{2,1,0:T(2,128)}) conditional(s32[]{:T(128)} %bitcast.9, (f32[2,40,128]{2,1,0:T(8,128)S(1)}, s32[3,40,128]{2,1,0:T(8,128)S(1)}, f32[8,128]{1,0:T(8,128)S(1)}, bf16[64,64]{1,0:T(8,128)(2,1)S(1)}, f32[128,1024]{1,0:T(8,128)S(1)}) %tuple.27, (s32[1,1]{1,0:T(1,128)}, f32[1,1,2,2048]{3,2,1,0:T(2,128)}, ...), branch_computations={%region_0.0_spmd, %region_1.6_spmd} | conditional | flops 334978816 | bytes 18040382 | solution.py:543
  19.9 1.7 %branch_0_fun.1 = f32[64,2,1024]{2,1,0:T(2,128)} custom-call(f32[2,40,128]{2,1,0:T(8,128)S(1)} %get-tuple-element.108.real, s32[3,40,128]{2,1,0:T(8,128)S(1)} %get-tuple-element.109.whole, f32[8,128]{1,0:T(8,128)S(1)} %get-tuple-element.110.number, bf16[64,64]{1,0:T(8,128)(2,1)S(1)} %get-tuple-element.111.table, f32[128,1024]{1,0:T(8,128)S(1)} %get-tuple-element.112.begun), custom_call_target="tpu_custom_call" | custom-call | tf_op jit(solution)/shard_map/cond/branch_0_fun/pallas_call | solution.py:530

commit v11 on v10

--- a/solution.py
+++ b/solution.py
@@ -344,14 +344,6 @@
             src_ref=ref.at[0:count], dst_ref=ref.at[0:count], send_sem=sent, recv_sem=landed,
             device_id=(t, lax.rem(c + 1, nc)), device_id_type=MESH)
 
-    all_of(tile_flags, nt - 1, tf_send, tf_recv).wait_recv()
-    chan_flags[c] = jnp.max(tile_flags[...], axis=0)
-
-    for i in range(1, nc):
-        pltpu.make_async_remote_copy(
-            src_ref=chan_flags.at[c], dst_ref=chan_flags.at[c], send_sem=cf_send, recv_sem=cf_recv,
-            device_id=(t, lax.rem(c + i, nc)), device_id_type=MESH).start()
-
     table[...] = class_table()
     total[...] = jnp.zeros_like(total)
 
@@ -409,6 +401,16 @@
     prepare(here, 0)
 
     def two_chips(j, carry):
+        @pl.when(j == 1)
+        def _():
+            all_of(tile_flags, nt - 1, tf_send, tf_recv).wait_recv()
+            chan_flags[c] = jnp.max(tile_flags[...], axis=0)
+
+            for i in range(1, nc):
+                pltpu.make_async_remote_copy(
+                    src_ref=chan_flags.at[c], dst_ref=chan_flags.at[c], send_sem=cf_send, recv_sem=cf_recv,
+                    device_id=(t, lax.rem(c + i, nc)), device_id_type=MESH).start()
+
         for odd in (1, 0):
             source = chip(2 * j + 2 - odd)
             arrive(source)

time: 21.8 us -> 22.4 us (1.028)
  the two profiles are of different devices: /device:TPU:8 before, /device:TPU:1 now
where the time goes in v11:
time: 22.4 us; the launch traced here: 22.2 us
  Pallas kernels  21 us (94%)
  between operations  1.22 us (5%)
    pallas_call x1, Pallas kernels, per_device(): pl.pallas_call(exchange, out_shape=(jax.ShapeDtypeStruct((2 * M, 4 * PLAN...  19.3 us
    pallas_call x1, Pallas kernels, usual(): pl.pallas_call(owned_rows, out_shape=jax.ShapeDtypeStruct((G // nc, 2, G)...  1.66 us

profile of v11, /device:TPU:1, one launch (start us, length us, event | category | flops | bytes accessed | tf_op | source)
XLA Modules:
  0.0 22.2 jit_solution(181034912446861456)
XLA Ops:
  0.7 19.3 %shard_map.57 = (bf16[64,64]{1,0:T(8,128)(2,1)S(1)}, f32[128,1024]{1,0:T(8,128)S(1)}, f32[2,40,128]{2,1,0:T(8,128)S(1)}, s32[3,40,128]{2,1,0:T(8,128)S(1)}, f32[8,128]{1,0:T(8,128)S(1)}, /*index=5*/s32[1,1]{1,0:T(1,128)}) custom-call(f32[1,1,2,2048]{3,2,1,0:T(2,128)} %vis.1, s32[1,1,2,2048]{3,2,1,0:T(2,128)} %cell.1, s32[1,1,2048]{2,1,0:T(1,128)} %sup.1, ...), custom_call_target="tpu_custom_call" | custom-call | tf_op jit(solution)/shard_map/pallas_call | solution.py:492
  20.5 1.7 %conditional.1 = (f32[64,2,1024]{2,1,0:T(2,128)}) conditional(s32[]{:T(128)} %bitcast.9, (f32[2,40,128]{2,1,0:T(8,128)S(1)}, s32[3,40,128]{2,1,0:T(8,128)S(1)}, f32[8,128]{1,0:T(8,128)S(1)}, bf16[64,64]{1,0:T(8,128)(2,1)S(1)}, f32[128,1024]{1,0:T(8,128)S(1)}) %tuple.27, (s32[1,1]{1,0:T(1,128)}, f32[1,1,2,2048]{3,2,1,0:T(2,128)}, ...), branch_computations={%region_0.0_spmd, %region_1.6_spmd} | conditional | flops 334978816 | bytes 18040382 | solution.py:545
  20.5 1.7 %branch_0_fun.1 = f32[64,2,1024]{2,1,0:T(2,128)} custom-call(f32[2,40,128]{2,1,0:T(8,128)S(1)} %get-tuple-element.108.real, s32[3,40,128]{2,1,0:T(8,128)S(1)} %get-tuple-element.109.whole, f32[8,128]{1,0:T(8,128)S(1)} %get-tuple-element.110.number, bf16[64,64]{1,0:T(8,128)(2,1)S(1)} %get-tuple-element.111.table, f32[128,1024]{1,0:T(8,128)S(1)} %get-tuple-element.112.begun), custom_call_target="tpu_custom_call" | custom-call | tf_op jit(solution)/shard_map/cond/branch_0_fun/pallas_call | solution.py:532

commit v12 on v10

--- a/solution.py
+++ b/solution.py
@@ -344,14 +344,6 @@
             src_ref=ref.at[0:count], dst_ref=ref.at[0:count], send_sem=sent, recv_sem=landed,
             device_id=(t, lax.rem(c + 1, nc)), device_id_type=MESH)
 
-    all_of(tile_flags, nt - 1, tf_send, tf_recv).wait_recv()
-    chan_flags[c] = jnp.max(tile_flags[...], axis=0)
-
-    for i in range(1, nc):
-        pltpu.make_async_remote_copy(
-            src_ref=chan_flags.at[c], dst_ref=chan_flags.at[c], send_sem=cf_send, recv_sem=cf_recv,
-            device_id=(t, lax.rem(c + i, nc)), device_id_type=MESH).start()
-
     table[...] = class_table()
     total[...] = jnp.zeros_like(total)
 
@@ -407,6 +399,14 @@
 
     arrive(here + (c + 1) % 2)
     prepare(here, 0)
+
+    all_of(tile_flags, nt - 1, tf_send, tf_recv).wait_recv()
+    chan_flags[c] = jnp.max(tile_flags[...], axis=0)
+
+    for i in range(1, nc):
+        pltpu.make_async_remote_copy(
+            src_ref=chan_flags.at[c], dst_ref=chan_flags.at[c], send_sem=cf_send, recv_sem=cf_recv,
+            device_id=(t, lax.rem(c + i, nc)), device_id_type=MESH).start()
 
     def two_chips(j, carry):
         for odd in (1, 0):

time: 21.8 us -> 21.1 us (0.968)
  Pallas kernels: 20.3 us -> 19.7 us
    pallas_call x1, Pallas kernels: 18.7 us -> 18 us  [per_device(): pl.pallas_call(exchange, out_shape=(jax.ShapeDtypeStruct((2 * M, 4 * PLAN...]
where the time goes in v12:
time: 21.1 us; the launch traced here: 20.9 us
  Pallas kernels  19.7 us (93%)
  between operations  1.22 us (6%)
    pallas_call x1, Pallas kernels, per_device(): pl.pallas_call(exchange, out_shape=(jax.ShapeDtypeStruct((2 * M, 4 * PLAN...  18 us
    pallas_call x1, Pallas kernels, usual(): pl.pallas_call(owned_rows, out_shape=jax.ShapeDtypeStruct((G // nc, 2, G)...  1.66 us

profile of v12, /device:TPU:8, one launch (start us, length us, event | category | flops | bytes accessed | tf_op | source)
XLA Modules:
  0.0 20.9 jit_solution(3354611818171880762)
XLA Ops:
  0.7 18.0 %shard_map.57 = (bf16[64,64]{1,0:T(8,128)(2,1)S(1)}, f32[128,1024]{1,0:T(8,128)S(1)}, f32[2,40,128]{2,1,0:T(8,128)S(1)}, s32[3,40,128]{2,1,0:T(8,128)S(1)}, f32[8,128]{1,0:T(8,128)S(1)}, /*index=5*/s32[1,1]{1,0:T(1,128)}) custom-call(f32[1,1,2,2048]{3,2,1,0:T(2,128)} %vis.1, s32[1,1,2,2048]{3,2,1,0:T(2,128)} %cell.1, s32[1,1,2048]{2,1,0:T(1,128)} %sup.1, ...), custom_call_target="tpu_custom_call" | custom-call | tf_op jit(solution)/shard_map/pallas_call | solution.py:490
  19.2 1.7 %conditional.1 = (f32[64,2,1024]{2,1,0:T(2,128)}) conditional(s32[]{:T(128)} %bitcast.9, (f32[2,40,128]{2,1,0:T(8,128)S(1)}, s32[3,40,128]{2,1,0:T(8,128)S(1)}, f32[8,128]{1,0:T(8,128)S(1)}, bf16[64,64]{1,0:T(8,128)(2,1)S(1)}, f32[128,1024]{1,0:T(8,128)S(1)}) %tuple.27, (s32[1,1]{1,0:T(1,128)}, f32[1,1,2,2048]{3,2,1,0:T(2,128)}, ...), branch_computations={%region_0.0_spmd, %region_1.6_spmd} | conditional | flops 334978816 | bytes 18040382 | solution.py:543
  19.2 1.7 %branch_0_fun.1 = f32[64,2,1024]{2,1,0:T(2,128)} custom-call(f32[2,40,128]{2,1,0:T(8,128)S(1)} %get-tuple-element.108.real, s32[3,40,128]{2,1,0:T(8,128)S(1)} %get-tuple-element.109.whole, f32[8,128]{1,0:T(8,128)S(1)} %get-tuple-element.110.number, bf16[64,64]{1,0:T(8,128)(2,1)S(1)} %get-tuple-element.111.table, f32[128,1024]{1,0:T(8,128)S(1)} %get-tuple-element.112.begun), custom_call_target="tpu_custom_call" | custom-call | tf_op jit(solution)/shard_map/cond/branch_0_fun/pallas_call | solution.py:530

commit v13 on v12

--- a/solution.py
+++ b/solution.py
@@ -212,11 +212,11 @@
     nt, nc = lax.axis_size("tile"), lax.axis_size("chan")
     slots = vis_v.shape[-1]
     loads = [
-        pltpu.make_async_copy(vis.at[0, 0], vis_v, load_sem.at[0]),
-        pltpu.make_async_copy(cell.at[0, 0], cell_v, load_sem.at[1]),
-        pltpu.make_async_copy(sup.at[0], sup_v, load_sem.at[2]),
-        pltpu.make_async_copy(wpl.at[0], wpl_v, load_sem.at[3]),
-        pltpu.make_async_copy(cnt, cnt_v, load_sem.at[4]),
+        pltpu.make_async_copy(cell.at[0, 0], cell_v, load_sem.at[0]),
+        pltpu.make_async_copy(cnt, cnt_v, load_sem.at[1]),
+        pltpu.make_async_copy(vis.at[0, 0], vis_v, load_sem.at[2]),
+        pltpu.make_async_copy(sup.at[0], sup_v, load_sem.at[3]),
+        pltpu.make_async_copy(wpl.at[0], wpl_v, load_sem.at[4]),
     ]
     for load in loads:
         load.start()
@@ -240,7 +240,7 @@
         for g in range(nc):
             pl.semaphore_signal(bar, inc=1, device_id=(t + 1, g), device_id_type=MESH)
 
-    for load in loads:
+    for load in loads[:2]:
         load.wait()
 
     live = lax.broadcasted_iota(jnp.int32, (1, slots), 1) < cnt_v[...]
@@ -278,6 +278,8 @@
         high = x.astype(BF16).astype(F32)
         return high, x - high
 
+    for load in loads[2:]:
+        load.wait()
     re_hi, re_lo = halves(vis_v[0:1])
     im_hi, im_lo = halves(vis_v[1:2])
     col = cell_v[1:2]

time: 21.1 us -> 21.1 us (level)
  no operation moved by 1% of the time
where the time goes in v13:
time: 21.1 us; the launch traced here: 20.9 us
  Pallas kernels  19.7 us (93%)
  between operations  1.22 us (6%)
    pallas_call x1, Pallas kernels, per_device(): pl.pallas_call(exchange, out_shape=(jax.ShapeDtypeStruct((2 * M, 4 * PLAN...  18 us
    pallas_call x1, Pallas kernels, usual(): pl.pallas_call(owned_rows, out_shape=jax.ShapeDtypeStruct((G // nc, 2, G)...  1.66 us

profile of v13, /device:TPU:8, one launch (start us, length us, event | category | flops | bytes accessed | tf_op | source)
XLA Modules:
  0.0 20.9 jit_solution(307905441824268918)
XLA Ops:
  0.7 18.0 %shard_map.57 = (bf16[64,64]{1,0:T(8,128)(2,1)S(1)}, f32[128,1024]{1,0:T(8,128)S(1)}, f32[2,40,128]{2,1,0:T(8,128)S(1)}, s32[3,40,128]{2,1,0:T(8,128)S(1)}, f32[8,128]{1,0:T(8,128)S(1)}, /*index=5*/s32[1,1]{1,0:T(1,128)}) custom-call(f32[1,1,2,2048]{3,2,1,0:T(2,128)} %vis.1, s32[1,1,2,2048]{3,2,1,0:T(2,128)} %cell.1, s32[1,1,2048]{2,1,0:T(1,128)} %sup.1, ...), custom_call_target="tpu_custom_call" | custom-call | tf_op jit(solution)/shard_map/pallas_call | solution.py:492
  19.2 1.7 %conditional.1 = (f32[64,2,1024]{2,1,0:T(2,128)}) conditional(s32[]{:T(128)} %bitcast.9, (f32[2,40,128]{2,1,0:T(8,128)S(1)}, s32[3,40,128]{2,1,0:T(8,128)S(1)}, f32[8,128]{1,0:T(8,128)S(1)}, bf16[64,64]{1,0:T(8,128)(2,1)S(1)}, f32[128,1024]{1,0:T(8,128)S(1)}) %tuple.27, (s32[1,1]{1,0:T(1,128)}, f32[1,1,2,2048]{3,2,1,0:T(2,128)}, ...), branch_computations={%region_0.0_spmd, %region_1.6_spmd} | conditional | flops 334978816 | bytes 18040382 | solution.py:545
  19.2 1.7 %branch_0_fun.1 = f32[64,2,1024]{2,1,0:T(2,128)} custom-call(f32[2,40,128]{2,1,0:T(8,128)S(1)} %get-tuple-element.108.real, s32[3,40,128]{2,1,0:T(8,128)S(1)} %get-tuple-element.109.whole, f32[8,128]{1,0:T(8,128)S(1)} %get-tuple-element.110.number, bf16[64,64]{1,0:T(8,128)(2,1)S(1)} %get-tuple-element.111.table, f32[128,1024]{1,0:T(8,128)S(1)} %get-tuple-element.112.begun), custom_call_target="tpu_custom_call" | custom-call | tf_op jit(solution)/shard_map/cond/branch_0_fun/pallas_call | solution.py:532

commit v14 on v12

--- a/solution.py
+++ b/solution.py
@@ -316,9 +316,6 @@
             src_ref=packed.at[pl.ds(pl.multiple_of(8 * peer, 8), width)], dst_ref=got.at[slot], send_sem=send_sem,
             recv_sem=recv_sem.at[slot], device_id=(t, peer), device_id_type=MESH)
 
-    for i in range(1, nc):
-        payload(i, c).start()
-
     def edge_up():
         return pltpu.make_async_remote_copy(
             src_ref=packed.at[pl.ds(buckets * GROUPS_IN, GROUPS_IN)], dst_ref=edge.at[c, 0:GROUPS_IN], send_sem=edge_send.at[0],
@@ -336,6 +333,9 @@
     @pl.when(t > 0)
     def _():
         edge_down().start()
+
+    for i in range(1, nc):
+        payload(i, c).start()
 
     got[c] = packed[pl.ds(pl.multiple_of(8 * c, 8), width), :]
 

time: 21.1 us -> 21.2 us (level)
  no operation moved by 1% of the time
where the time goes in v14:
time: 21.2 us; the launch traced here: 20.9 us
  Pallas kernels  19.7 us (93%)
  between operations  1.22 us (6%)
    pallas_call x1, Pallas kernels, per_device(): pl.pallas_call(exchange, out_shape=(jax.ShapeDtypeStruct((2 * M, 4 * PLAN...  18 us
    pallas_call x1, Pallas kernels, usual(): pl.pallas_call(owned_rows, out_shape=jax.ShapeDtypeStruct((G // nc, 2, G)...  1.66 us

profile of v14, /device:TPU:8, one launch (start us, length us, event | category | flops | bytes accessed | tf_op | source)
XLA Modules:
  0.0 20.9 jit_solution(4700067499412799330)
XLA Ops:
  0.7 18.0 %shard_map.57 = (bf16[64,64]{1,0:T(8,128)(2,1)S(1)}, f32[128,1024]{1,0:T(8,128)S(1)}, f32[2,40,128]{2,1,0:T(8,128)S(1)}, s32[3,40,128]{2,1,0:T(8,128)S(1)}, f32[8,128]{1,0:T(8,128)S(1)}, /*index=5*/s32[1,1]{1,0:T(1,128)}) custom-call(f32[1,1,2,2048]{3,2,1,0:T(2,128)} %vis.1, s32[1,1,2,2048]{3,2,1,0:T(2,128)} %cell.1, s32[1,1,2048]{2,1,0:T(1,128)} %sup.1, ...), custom_call_target="tpu_custom_call" | custom-call | tf_op jit(solution)/shard_map/pallas_call | solution.py:490
  19.2 1.7 %conditional.1 = (f32[64,2,1024]{2,1,0:T(2,128)}) conditional(s32[]{:T(128)} %bitcast.9, (f32[2,40,128]{2,1,0:T(8,128)S(1)}, s32[3,40,128]{2,1,0:T(8,128)S(1)}, f32[8,128]{1,0:T(8,128)S(1)}, bf16[64,64]{1,0:T(8,128)(2,1)S(1)}, f32[128,1024]{1,0:T(8,128)S(1)}) %tuple.27, (s32[1,1]{1,0:T(1,128)}, f32[1,1,2,2048]{3,2,1,0:T(2,128)}, ...), branch_computations={%region_0.0_spmd, %region_1.6_spmd} | conditional | flops 334978816 | bytes 18040382 | solution.py:543
  19.3 1.7 %branch_0_fun.1 = f32[64,2,1024]{2,1,0:T(2,128)} custom-call(f32[2,40,128]{2,1,0:T(8,128)S(1)} %get-tuple-element.108.real, s32[3,40,128]{2,1,0:T(8,128)S(1)} %get-tuple-element.109.whole, f32[8,128]{1,0:T(8,128)S(1)} %get-tuple-element.110.number, bf16[64,64]{1,0:T(8,128)(2,1)S(1)} %get-tuple-element.111.table, f32[128,1024]{1,0:T(8,128)S(1)} %get-tuple-element.112.begun), custom_call_target="tpu_custom_call" | custom-call | tf_op jit(solution)/shard_map/cond/branch_0_fun/pallas_call | solution.py:530
